TPU v7x, 32 devices: a whole 2x2x4 slice. The times are simulated.
32 devices in a mesh: dp: 16 (over z, y, core), seq: 2 (over x).
Axes of the slice: x: 2, y: 2, z: 4, core: 2. Of those that a mesh axis runs over, the one named last changes fastest.
Arguments:
- token_ids: int32 [16, 1024], P('dp'), may hold values from 0 to 31999
- segment_ids: int32 [16, 1024], P('dp'), may hold values from 0 to 7, never falling along the last dimension, each value on 1 to 512 neighbouring positions
- time_steps: int32 [16], P('dp'), may hold values from 0 to 999
- row_seeds: int32 [16], P('dp'), may hold values from 0 to 65520
- loss_weights: float32 [16, 1024], P('dp', 'seq'), may hold values from -6 to 6
- embed_table: bfloat16 [32000, 256], P(('dp', 'seq')), may hold values from -6 to 6
- input_proj: bfloat16 [256, 1024], P(('dp', 'seq')), may hold values from -0.375 to 0.375
- attn_gain: bfloat16 [1024], P(('dp', 'seq')), may hold values from 0.5 to 1.5
- attn_bias: bfloat16 [1024], P(('dp', 'seq')), may hold values from -1.796875 to 1.796875
- qkv_proj: bfloat16 [1024, 3072], P(('dp', 'seq')), may hold values from -0.1875 to 0.1875
- attn_proj: bfloat16 [1024, 1024], P(('dp', 'seq')), may hold values from -0.75 to 0.75
- mlp_gain: bfloat16 [1024], P(('dp', 'seq')), may hold values from 0.5 to 1.5
- mlp_bias: bfloat16 [1024], P(('dp', 'seq')), may hold values from -1.796875 to 1.796875
- up_proj: bfloat16 [1024, 4096], P(('dp', 'seq')), may hold values from -0.1875 to 0.1875
- up_bias: bfloat16 [4096], P(('dp', 'seq')), may hold values from -1.796875 to 1.796875
- down_proj: bfloat16 [4096, 1024], P(('dp', 'seq')), may hold values from -0.09375 to 0.09375
- output_proj: bfloat16 [1024, 256], P(('dp', 'seq')), may hold values from -0.1875 to 0.1875
Outputs:
- token_loss: float32 [16, 1024], P('dp', 'seq')
- table_grad: float32 [32000, 256], P(('dp', 'seq'))
- input_proj_grad: float32 [256, 1024], P(('dp', 'seq'))
- attn_gain_grad: float32 [1024], P(('dp', 'seq'))
- attn_bias_grad: float32 [1024], P(('dp', 'seq'))
- qkv_proj_grad: float32 [1024, 3072], P(('dp', 'seq'))
- attn_proj_grad: float32 [1024, 1024], P(('dp', 'seq'))
- mlp_gain_grad: float32 [1024], P(('dp', 'seq'))
- mlp_bias_grad: float32 [1024], P(('dp', 'seq'))
- up_proj_grad: float32 [1024, 4096], P(('dp', 'seq'))
- up_bias_grad: float32 [4096], P(('dp', 'seq'))
- down_proj_grad: float32 [4096, 1024], P(('dp', 'seq'))
- output_proj_grad: float32 [1024, 256], P(('dp', 'seq'))
Inputs may be any that keep to these rules, and one draw needn't show every extreme that they name: `token_ids`: token ids over the vocabulary; a few of them are very common. `segment_ids`: within a row the ids never fall, so each document is one run of positions of at most 512; the longest run in a draw has exactly 512 positions.
All inputs are finite; a program needn't handle non-finite values.
Results may differ from a plain program's by a relative error of at most 0.015.
Values may be sent and summed in bfloat16 or wider, within the bound.
No kernel may reach another device: no remote copies, remote signals or barrier semaphores. Data moves between devices by JAX's collectives and lax.ppermute only.
A program may use at most 256 MiB of HBM per device.

v0:
```python
import math

import jax
import jax.numpy as jnp
from jax import lax
from jax.sharding import PartitionSpec as P

D = 1024
HEAD_DIM = 64
TSTEPS = 1000


def combined_all(shard, axis, combine):
    everything = jax.tree.map(lambda part: lax.all_gather(part, axis), shard)
    first = jax.tree.map(lambda part: part[0], everything)

    def step(k, so_far):
        return combine(so_far, jax.tree.map(lambda part: part[k], everything))

    return lax.fori_loop(1, lax.axis_size(axis), step, first)


def product(left, right):
    return jnp.dot(left, right, preferred_element_type=jnp.float32)


def product_left(left, right):
    return lax.dot_general(
        left, right, (((0,), (0,)), ((), ())), preferred_element_type=jnp.float32
    )


def product_right(left, right):
    return lax.dot_general(
        left, right, (((1,), (1,)), ((), ())), preferred_element_type=jnp.float32
    )


def normalize_rows(matrix):
    return matrix * lax.rsqrt(jnp.mean(matrix * matrix, axis=1, keepdims=True) + 1e-06)


def layer_norm(hidden, norm_gain, norm_bias):
    centre = hidden - jnp.mean(hidden, axis=-1, keepdims=True)
    spread = jnp.mean(centre * centre, axis=-1, keepdims=True)
    return centre * lax.rsqrt(spread + 1e-05) * norm_gain + norm_bias


def exact_gelu(pre_act):
    return jax.nn.gelu(pre_act, approximate=False)


def noise_field(row_seeds, positions, channel_count):
    channel = lax.iota(jnp.int32, channel_count)
    mixed_once = (
        row_seeds[:, None, None] + 7919 * positions[None, :, None] + 104729 * channel[None, None, :]
    ) % 65521
    mixed_twice = (mixed_once * (mixed_once % 32719) + 31 * channel[None, None, :]) % 65521
    return (mixed_twice.astype(jnp.float32) / 32760.5 - 1.0) * 1.7320508


def time_terms(time_steps):
    fraction = time_steps.astype(jnp.float32) / (TSTEPS - 1)
    noise_level = 0.3 * jnp.exp(fraction * math.log(30.0))
    return (noise_level, lax.rsqrt(1.0 + noise_level * noise_level), 0.5 + fraction)


def masked_scores(query_block, key_rows, segment_block, segment_row):
    scores = jnp.einsum("qhd,khd->hqk", query_block, key_rows, preferred_element_type=jnp.float32)
    same_doc = segment_block[:, None] == segment_row[None, :]
    return jnp.where(same_doc[None], scores, -1e30)


def attend_row(operands):
    queries, key_rows, value_rows, segment_row = operands
    length = queries.shape[0]
    block_rows = math.gcd(length, 512)
    block_count = length // block_rows

    def attend_block(pieces):
        query_block, segment_block = pieces
        scores = masked_scores(query_block, key_rows, segment_block, segment_row)
        row_max = jnp.max(scores, axis=-1, keepdims=True)
        raised = jnp.exp(scores - row_max)
        summed = jnp.sum(raised, axis=-1, keepdims=True)
        probs_low = (raised / summed).astype(jnp.bfloat16)
        attended = jnp.einsum(
            "hqk,khd->qhd", probs_low, value_rows, preferred_element_type=jnp.float32
        )
        return (attended.astype(jnp.bfloat16), (row_max + jnp.log(summed))[..., 0])

    attended, log_total = lax.map(
        attend_block,
        (
            queries.reshape((block_count, block_rows) + queries.shape[1:]),
            segment_row.reshape(block_count, block_rows),
        ),
    )
    return (attended.reshape(queries.shape), log_total)


def attend_back_row(operands):
    queries, key_rows, value_rows, segment_row, grad_rows, log_total = operands
    length = queries.shape[0]
    block_rows = math.gcd(length, 512)
    block_count = length // block_rows

    def back_block(carry, pieces):
        key_sum, value_sum = carry
        query_block, segment_block, grad_block, total_block = pieces
        scores = masked_scores(query_block, key_rows, segment_block, segment_row)
        probs = jnp.exp(scores - total_block[:, :, None])
        prob_grad = jnp.einsum(
            "qhd,khd->hqk", grad_block, value_rows, preferred_element_type=jnp.float32
        )
        score_grad = (
            probs * (prob_grad - jnp.sum(probs * prob_grad, axis=-1, keepdims=True))
        ).astype(jnp.bfloat16)
        query_grad = jnp.einsum(
            "hqk,khd->qhd", score_grad, key_rows, preferred_element_type=jnp.float32
        )
        key_sum = key_sum + jnp.einsum(
            "hqk,qhd->khd", score_grad, query_block, preferred_element_type=jnp.float32
        )
        value_sum = value_sum + jnp.einsum(
            "hqk,qhd->khd",
            probs.astype(jnp.bfloat16),
            grad_block,
            preferred_element_type=jnp.float32,
        )
        return ((key_sum, value_sum), query_grad.astype(jnp.bfloat16))

    block_shape = (block_count, block_rows) + queries.shape[1:]
    start_sums = (jnp.zeros(key_rows.shape, jnp.float32), jnp.zeros(value_rows.shape, jnp.float32))
    (key_sum, value_sum), query_grad = lax.scan(
        back_block,
        start_sums,
        (
            queries.reshape(block_shape),
            segment_row.reshape(block_count, block_rows),
            grad_rows.reshape(block_shape),
            log_total,
        ),
    )
    return (
        query_grad.reshape(queries.shape),
        key_sum.astype(jnp.bfloat16),
        value_sum.astype(jnp.bfloat16),
    )


def join_parts(first, second):
    top = jnp.maximum(first[0], second[0])
    total = first[1] * jnp.exp(first[0] - top) + second[1] * jnp.exp(second[0] - top)
    return (top, total, first[2] + second[2], first[3] + second[3])


def local(
    token_ids,
    segment_ids,
    time_steps,
    row_seeds,
    loss_weights,
    embed_table,
    input_proj,
    attn_gain,
    attn_bias,
    qkv_proj,
    attn_proj,
    mlp_gain,
    mlp_bias,
    up_proj,
    up_bias,
    down_proj,
    output_proj,
):
    seq_count = lax.axis_size("seq")
    seq_place = lax.axis_index("seq")
    dp_count = lax.axis_size("dp")
    row_count, length = token_ids.shape
    local_len = length // seq_count
    tok_count = row_count * local_len
    start_pos = seq_place * local_len
    own_ids = lax.dynamic_slice_in_dim(token_ids, start_pos, local_len, 1)
    positions = start_pos + lax.iota(jnp.int32, local_len)
    gathered = (
        lax.all_gather(embed_table, ("dp", "seq"), axis=0, tiled=True),
        lax.all_gather(input_proj, ("dp", "seq"), axis=0, tiled=True),
        lax.all_gather(attn_gain, ("dp", "seq"), axis=0, tiled=True),
        lax.all_gather(attn_bias, ("dp", "seq"), axis=0, tiled=True),
        lax.all_gather(qkv_proj, ("dp", "seq"), axis=0, tiled=True),
        lax.all_gather(attn_proj, ("dp", "seq"), axis=0, tiled=True),
        lax.all_gather(mlp_gain, ("dp", "seq"), axis=0, tiled=True),
        lax.all_gather(mlp_bias, ("dp", "seq"), axis=0, tiled=True),
        lax.all_gather(up_proj, ("dp", "seq"), axis=0, tiled=True),
        lax.all_gather(up_bias, ("dp", "seq"), axis=0, tiled=True),
        lax.all_gather(down_proj, ("dp", "seq"), axis=0, tiled=True),
        lax.all_gather(output_proj, ("dp", "seq"), axis=0, tiled=True),
    )
    (
        table_full,
        input_full,
        gain_one,
        bias_one,
        qkv_full,
        attn_full,
        gain_two,
        bias_two,
        up_full,
        upbias_full,
        down_full,
        output_full,
    ) = gathered
    vocab_size, embed_width = table_full.shape
    block_len = vocab_size // (dp_count * seq_count)
    unit, unit_back = jax.vjp(normalize_rows, table_full.astype(jnp.float32))
    sub_table = lax.dynamic_slice_in_dim(
        table_full.reshape(dp_count, seq_count, block_len, embed_width), seq_place, 1, 1
    ).reshape(dp_count * block_len, embed_width)
    sub_unit = lax.dynamic_slice_in_dim(
        unit.reshape(dp_count, seq_count, block_len, embed_width), seq_place, 1, 1
    ).reshape(dp_count * block_len, embed_width)
    scaled = (sub_unit * embed_width ** (-0.5)).astype(jnp.bfloat16)
    local_rows = lax.iota(jnp.int32, dp_count * block_len)
    vocab_index = (
        local_rows // block_len * seq_count + seq_place
    ) * block_len + local_rows % block_len
    noise_level, input_scale, residual_scale = time_terms(time_steps)
    noise = noise_field(row_seeds, positions, embed_width)
    embedded = jnp.take(unit, own_ids, axis=0)
    inputs = (
        (input_scale[:, None, None] * (embedded + noise_level[:, None, None] * noise))
        .astype(jnp.bfloat16)
        .reshape(tok_count, embed_width)
    )
    token_scale = jnp.repeat(residual_scale, local_len)[:, None]
    token_input_scale = jnp.repeat(input_scale, local_len)[:, None]
    hidden_zero = product(inputs, input_full)
    first_norm, first_back = jax.vjp(
        layer_norm, hidden_zero, gain_one.astype(jnp.float32), bias_one.astype(jnp.float32)
    )
    first_in = first_norm.astype(jnp.bfloat16)
    qkv = product(first_in, qkv_full)
    query_tok = (
        (qkv[:, :D] * HEAD_DIM ** (-0.5)).astype(jnp.bfloat16).reshape(row_count, local_len, D)
    )
    key_tok = qkv[:, D : 2 * D].astype(jnp.bfloat16).reshape(row_count, local_len, D)
    value_tok = qkv[:, 2 * D :].astype(jnp.bfloat16).reshape(row_count, local_len, D)
    head_q, head_k, head_v = (
        lax.all_to_all(query_tok, "seq", split_axis=2, concat_axis=1, tiled=True),
        lax.all_to_all(key_tok, "seq", split_axis=2, concat_axis=1, tiled=True),
        lax.all_to_all(value_tok, "seq", split_axis=2, concat_axis=1, tiled=True),
    )
    heads_here = head_q.shape[2] // HEAD_DIM
    head_shape = (row_count, length, heads_here, HEAD_DIM)
    head_q = head_q.reshape(head_shape)
    head_k = head_k.reshape(head_shape)
    head_v = head_v.reshape(head_shape)
    attended, log_total = lax.map(attend_row, (head_q, head_k, head_v, segment_ids))
    attended = attended.reshape(row_count, length, heads_here * HEAD_DIM)
    mixed = lax.all_to_all(attended, "seq", split_axis=1, concat_axis=2, tiled=True).reshape(
        tok_count, D
    )
    hidden_one = hidden_zero + token_scale * product(mixed, attn_full)
    second_norm, second_back = jax.vjp(
        layer_norm, hidden_one, gain_two.astype(jnp.float32), bias_two.astype(jnp.float32)
    )
    second_in = second_norm.astype(jnp.bfloat16)
    pre_act = product(second_in, up_full) + upbias_full.astype(jnp.float32)
    activated, gelu_back = jax.vjp(exact_gelu, pre_act)
    act_low = activated.astype(jnp.bfloat16)
    hidden_two = hidden_one + token_scale * product(act_low, down_full)
    final_in = hidden_two.astype(jnp.bfloat16)
    outputs = product(final_in, output_full).astype(jnp.bfloat16)
    group_tok = seq_count * tok_count
    group_out = lax.all_gather(outputs, "seq", axis=0, tiled=True)
    group_ids = (
        token_ids.reshape(row_count, seq_count, local_len).transpose(1, 0, 2).reshape(group_tok)
    )
    spread = jnp.where(
        lax.iota(jnp.int32, seq_count)[:, None] == seq_place,
        loss_weights.reshape(1, tok_count),
        0.0,
    )
    tile_rows = math.gcd(group_tok, 512)
    tile_count = group_tok // tile_rows
    out_tiles = group_out.reshape(tile_count, tile_rows, embed_width)
    id_tiles = group_ids.reshape(tile_count, tile_rows)

    def part_tile(pieces):
        out_block, target_block = pieces
        logits = product_right(out_block, scaled)
        row_max = jnp.max(logits, axis=1)
        exp_sum = jnp.sum(jnp.exp(logits - row_max[:, None]), axis=1)
        picked = jnp.sum(
            jnp.where(vocab_index[None, :] == target_block[:, None], logits, 0.0), axis=1
        )
        return (row_max, exp_sum, picked)

    part_max, part_sum, part_pick = lax.map(part_tile, (out_tiles, id_tiles))
    top, total, pick, weight_tiles = combined_all(
        (part_max, part_sum, part_pick, spread), "seq", join_parts
    )
    log_tiles = top + jnp.log(total)
    all_loss = log_tiles - pick
    token_loss = lax.dynamic_slice_in_dim(all_loss, seq_place, 1, 0)

    def back_tile(scaled_sum, pieces):
        out_block, target_block, log_block, weight_block = pieces
        logits = product_right(out_block, scaled)
        probs = jnp.exp(logits - log_block[:, None])
        onehot = (vocab_index[None, :] == target_block[:, None]).astype(jnp.float32)
        grad_logits = (weight_block[:, None] * (probs - onehot)).astype(jnp.bfloat16)
        scaled_sum = scaled_sum + product_left(grad_logits, out_block)
        return (scaled_sum, product(grad_logits, scaled))

    scaled_grad, out_terms = lax.scan(
        back_tile,
        jnp.zeros(scaled.shape, jnp.float32),
        (out_tiles, id_tiles, log_tiles, weight_tiles),
    )
    out_terms = out_terms.reshape(tile_count * tile_rows, embed_width)
    out_grad = lax.psum_scatter(out_terms, "seq", scatter_dimension=0, tiled=True).astype(
        jnp.bfloat16
    )
    output_w_grad = product_left(final_in, out_grad)
    hidden_two_grad = product_right(out_grad, output_full)
    branch_grad = (token_scale * hidden_two_grad).astype(jnp.bfloat16)
    down_w_grad = product_left(act_low, branch_grad)
    pre_grad = gelu_back(product_right(branch_grad, down_full))[0].astype(jnp.bfloat16)
    up_w_grad = product_left(second_in, pre_grad)
    upbias_grad = jnp.sum(pre_grad, axis=0, dtype=jnp.float32)
    hidden_one_part, gain_two_grad, bias_two_grad = second_back(product_right(pre_grad, up_full))
    hidden_one_grad = hidden_two_grad + hidden_one_part
    attn_grad = (token_scale * hidden_one_grad).astype(jnp.bfloat16)
    attn_w_grad = product_left(mixed, attn_grad)
    mixed_grad = (
        product_right(attn_grad, attn_full).astype(jnp.bfloat16).reshape(row_count, local_len, D)
    )
    head_grad = lax.all_to_all(mixed_grad, "seq", split_axis=2, concat_axis=1, tiled=True).reshape(
        head_shape
    )
    query_grad, key_grad, value_grad = lax.map(
        attend_back_row, (head_q, head_k, head_v, segment_ids, head_grad, log_total)
    )
    merged_shape = (row_count, length, heads_here * HEAD_DIM)
    query_back, key_back, value_back = (
        lax.all_to_all(
            query_grad.reshape(merged_shape), "seq", split_axis=1, concat_axis=2, tiled=True
        ),
        lax.all_to_all(
            key_grad.reshape(merged_shape), "seq", split_axis=1, concat_axis=2, tiled=True
        ),
        lax.all_to_all(
            value_grad.reshape(merged_shape), "seq", split_axis=1, concat_axis=2, tiled=True
        ),
    )
    qkv_grad = jnp.concatenate(
        [query_back * HEAD_DIM ** (-0.5), key_back, value_back], axis=2
    ).reshape(tok_count, 3 * D)
    qkv_w_grad = product_left(first_in, qkv_grad)
    hidden_zero_part, gain_one_grad, bias_one_grad = first_back(product_right(qkv_grad, qkv_full))
    hidden_zero_grad = (hidden_one_grad + hidden_zero_part).astype(jnp.bfloat16)
    input_w_grad = product_left(inputs, hidden_zero_grad)
    embedded_grad = token_input_scale * product_right(hidden_zero_grad, input_full)
    scaled_part = scaled_grad * embed_width ** (-0.5)
    group_grad = lax.all_gather(
        embedded_grad.astype(jnp.bfloat16), "seq", axis=0, tiled=True
    ).astype(embedded_grad.dtype)
    block_id = group_ids // block_len
    owned = block_id % seq_count == seq_place
    local_slot = jnp.where(
        owned, block_id // seq_count * block_len + group_ids % block_len, scaled.shape[0]
    )
    unit_grad = scaled_part.at[local_slot].add(group_grad, mode="drop")
    table_term = jax.vjp(normalize_rows, sub_table.astype(jnp.float32))[1](unit_grad)[0]
    table_grad = lax.psum_scatter(
        table_term.astype(jnp.bfloat16), "dp", scatter_dimension=0, tiled=True
    ).astype(jnp.float32)
    summed = (
        lax.psum_scatter(input_w_grad, ("dp", "seq"), scatter_dimension=0, tiled=True),
        lax.psum_scatter(gain_one_grad, ("dp", "seq"), scatter_dimension=0, tiled=True),
        lax.psum_scatter(bias_one_grad, ("dp", "seq"), scatter_dimension=0, tiled=True),
        lax.psum_scatter(qkv_w_grad, ("dp", "seq"), scatter_dimension=0, tiled=True),
        lax.psum_scatter(attn_w_grad, ("dp", "seq"), scatter_dimension=0, tiled=True),
        lax.psum_scatter(gain_two_grad, ("dp", "seq"), scatter_dimension=0, tiled=True),
        lax.psum_scatter(bias_two_grad, ("dp", "seq"), scatter_dimension=0, tiled=True),
        lax.psum_scatter(up_w_grad, ("dp", "seq"), scatter_dimension=0, tiled=True),
        lax.psum_scatter(upbias_grad, ("dp", "seq"), scatter_dimension=0, tiled=True),
        lax.psum_scatter(down_w_grad, ("dp", "seq"), scatter_dimension=0, tiled=True),
        lax.psum_scatter(output_w_grad, ("dp", "seq"), scatter_dimension=0, tiled=True),
    )
    return (token_loss.reshape(row_count, local_len), table_grad) + tuple(summed)


def solution(mesh):
    in_specs = (
        P("dp", None),
        P("dp", None),
        P("dp"),
        P("dp"),
        P("dp", "seq"),
        P(("dp", "seq"), None),
        P(("dp", "seq"), None),
        P(("dp", "seq")),
        P(("dp", "seq")),
        P(("dp", "seq"), None),
        P(("dp", "seq"), None),
        P(("dp", "seq")),
        P(("dp", "seq")),
        P(("dp", "seq"), None),
        P(("dp", "seq")),
        P(("dp", "seq"), None),
        P(("dp", "seq"), None),
    )
    out_specs = (
        P("dp", "seq"),
        P(("dp", "seq"), None),
        P(("dp", "seq"), None),
        P(("dp", "seq")),
        P(("dp", "seq")),
        P(("dp", "seq"), None),
        P(("dp", "seq"), None),
        P(("dp", "seq")),
        P(("dp", "seq")),
        P(("dp", "seq"), None),
        P(("dp", "seq")),
        P(("dp", "seq"), None),
        P(("dp", "seq"), None),
    )
    return jax.shard_map(local, mesh=mesh, in_specs=in_specs, out_specs=out_specs, check_vma=False)
```

profile of v0, /device:TPU:0, one launch (start us, length us, event | category | flops | bytes accessed | tf_op | source)
XLA Modules:
  0.0 2505.7 jit_solution(5271815450546134838)
XLA Ops:
  14.7 43.3 %all-reduce.10 = (bf16[1024]{0:T(1024)(128)(2,1)S(1)}, bf16[1024]{0:T(1024)(128)(2,1)S(1)}, bf16[1024]{0:T(1024)(128)(2,1)S(1)}, bf16[1024]{0:T(1024)(128)(2,1)S(1)}) all-reduce(bf16[1024]{0:T(1024)(128)(2,1)S(1)} %dynamic-update-slice.1, bf16[1024]{0:T(1024)(128)(2,1)S(1)} %dynamic-update-slice, ...), channel_id=1, replica_groups=mesh['dp'=16,'seq'=2] {'dp','seq'}, use_global_device_ids=true, to_apply=%add.1 | all-reduce | flops 4096 | bytes 16384
  58.8 73.8 %all_gather.65 = bf16[256,1024]{1,0:T(8,128)(2,1)S(1)} all-gather(bf16[8,1024]{1,0:T(8,128)(2,1)} %param.31), channel_id=1, replica_groups=mesh['dp'=16,'seq'=2] {'dp','seq'}, dimensions={0}, use_global_device_ids=true | all-gather | bytes 540672 | tf_op jit(solution)/shard_map/all_gather | solution.py:188
  145.0 15.9 convert_multiply_fusion
  175.7 29.4 %all-gather.15.cloned.1.call-done = bf16[1024,3072]{1,0:T(8,128)(2,1)} async-done(((bf16[32,3072]{1,0:T(8,128)(2,1)}), bf16[1024,3072]{1,0:T(8,128)(2,1)}) %all-gather.15.cloned.1.call-update) | async-done | bytes 6291472 | tf_op jit(solution)/shard_map/all_gather | solution.py:191
  273.7 72.0 %all-gather.3 = bf16[32,1,128]{2,1,0:T(2,128)(2,1)S(1)} all-gather(bf16[1,1,128]{2,1,0:T(2,128)(2,1)S(1)} %bitcast.370), channel_id=1, replica_groups=mesh['dp'=16,'seq'=2] {'dp','seq'}, dimensions={0}, use_global_device_ids=true | all-gather | bytes 8448 | tf_op jit(solution)/shard_map/all_gather | solution.py:196
  353.0 74.4 %all_gather.75 = bf16[1024,256]{1,0:T(8,128)(2,1)} all-gather(bf16[32,256]{1,0:T(8,128)(2,1)S(1)} %copy-done.56), channel_id=1, replica_groups=mesh['dp'=16,'seq'=2] {'dp','seq'}, dimensions={0}, use_global_device_ids=true | all-gather | bytes 540672 | tf_op jit(solution)/shard_map/all_gather | solution.py:198
  447.7 25.7 %while.83 = (s32[]{:T(128)}, bf16[2,512,8,64]{1,3,2,0:T(8,128)(2,1)}, f32[2,8,512]{2,1,0:T(8,128)S(1)}, s32[2,512]{1,0:T(2,128)S(1)}, s32[1024]{0:T(1024)S(1)}, ...) while((s32[]{:T(128)}, ...), condition=%wide.region_6.7_spmd, body=%wide.region_3.6_spmd.sunk | while | flops 1112272896 | bytes 64104620 | solution.py:92
  522.7 27.6 %multiply_convert_fusion.3 = (bf16[512,4096]{1,0:T(8,128)(2,1)}, f32[512,4096]{1,0:T(8,128)}, f32[512,4096]{1,0:T(8,128)}) fusion(f32[4096]{0:T(1024)S(1)} %bitcast.362, bf16[1024,4096]{1,0:T(8,128)(2,1)} %all-gather.19.cloned.1.call-done, f32[512,1024]{1,0:T(8,128)S(1)} %get-tuple-element.500, f32[1024]{0:T(1024)S(1)} %copy-done.75, ...), kind=kOutput, calls=%fused_computation.113 | convolution fusion | flops 4436000768 | bytes 31485952 | tf_op jit(solution)/shard_map/dot_general | solution.py:24
  567.8 68.0 %while.84 = (s32[]{:T(128)}, f32[2,512]{1,0:T(2,128)S(1)}, f32[2,512]{1,0:T(2,128)S(1)}, f32[2,512]{1,0:T(2,128)}, bf16[2,512,256]{2,1,0:T(8,128)(2,1)S(1)}, /*i...) while((s32[]{:T(128)}, f32[2,512]{1,0:T(2,128)S(1)}, ...), condition=%wide.region_13.14_spmd.clone, body=%wide.region_9.13_spmd.clone.sunk | while | flops 4243710464 | bytes 74144888 | solution.py:300
  567.8 16.2 fusion.205
  584.1 16.4 select_reduce_fusion.5
  601.8 16.2 fusion.205
  618.1 16.4 select_reduce_fusion.5
  644.5 96.6 %while.85 = (s32[]{:T(128)}, f32[16000,256]{1,0:T(8,128)}, f32[2,512,256]{2,1,0:T(8,128)}, f32[2,512]{1,0:T(2,128)S(1)}, bf16[2,512,256]{2,1,0:T(8,128)(2,1)S(1)...) while((s32[]{:T(128)}, f32[16000,256]{1,0:T(8,128)}, ...), condition=%wide.region_15.16_spmd.clone, body=%wide.region_14.15_spmd.clone.sunk | while | flops 12640512000 | bytes 99500688 | solution.py:317
  644.6 17.0 multiply_convert_fusion.14
  661.6 15.7 convolution_add_fusion.2
  677.3 13.2 fusion.214
  690.6 16.9 multiply_convert_fusion.14
  707.5 20.4 convolution_add_fusion.2
  727.9 13.2 fusion.214
  741.1 19.1 reduce-scatter.9.cloned.1.call-done
  761.8 15.1 convert_reduce_fusion
  811.8 14.0 all-to-all-done.4
  830.1 104.9 %while.86 = (s32[]{:T(128)}, f32[1024,8,64]{0,2,1:T(8,128)}, f32[1024,8,64]{0,2,1:T(8,128)}, bf16[2,512,8,64]{1,3,2,0:T(8,128)(2,1)}, bf16[2,512,8,64]{1,3,2,0:T...) while((s32[]{:T(128)}, f32[1024,8,64]{0,2,1:T(8,128)}, ...), condition=%wide.region_21.22_spmd.clone, body=%wide.region_19.21_spmd.clone.sunk | while | flops 2737565696 | bytes 295430464 | solution.py:135
  1051.4 17.3 scatter_custom_fusion
  1151.0 40.9 %all-reduce.9 = (f32[1024]{0:T(1024)S(1)}, f32[1024]{0:T(1024)S(1)}, f32[1024]{0:T(1024)S(1)}, f32[1024]{0:T(1024)S(1)}, f32[4096]{0:T(1024)S(1)}) all-reduce(f32[1024]{0:T(1024)S(1)} %get-tuple-element.390, f32[1024]{0:T(1024)S(1)} %get-tuple-element.393, ...), channel_id=8, replica_groups=mesh['dp'=16,'seq'=2] {'dp','seq'}, use_global_device_ids=true, to_apply=%region_30.31.clone | all-reduce | flops 8192 | bytes 65536
  1207.5 134.8 %reduce-scatter.23.cloned.1.call-done = f32[32,256]{1,0:T(8,128)} async-done(((f32[1024,256]{1,0:T(8,128)}), f32[32,256]{1,0:T(8,128)}) %reduce-scatter.23.cloned.1.call-update) | async-done | bytes 32784 | tf_op jit(solution)/shard_map/reduce_scatter | solution.py:391
  1342.3 134.0 %reduce-scatter.13.cloned.1.call-done = f32[8,1024]{1,0:T(8,128)} async-done(((f32[256,1024]{1,0:T(8,128)}), f32[8,1024]{1,0:T(8,128)}) %reduce-scatter.13.cloned.1.call-update) | async-done | bytes 32784 | tf_op jit(solution)/shard_map/reduce_scatter | solution.py:381
  1476.2 140.9 %reduce-scatter.17.cloned.1.call-done = f32[32,1024]{1,0:T(8,128)} async-done(((f32[1024,1024]{1,0:T(8,128)}), f32[32,1024]{1,0:T(8,128)}) %reduce-scatter.17.cloned.1.call-update) | async-done | bytes 131088 | tf_op jit(solution)/shard_map/reduce_scatter | solution.py:385
  1617.1 160.8 %reduce-scatter.15.cloned.1.call-done = f32[32,3072]{1,0:T(8,128)} async-done(((f32[1024,3072]{1,0:T(8,128)}), f32[32,3072]{1,0:T(8,128)}) %reduce-scatter.15.cloned.1.call-update) | async-done | bytes 393232 | tf_op jit(solution)/shard_map/reduce_scatter | solution.py:384
  1778.0 359.2 %reduce-scatter.19.cloned.1.call-done = f32[32,4096]{1,0:T(8,128)} async-done(((f32[1024,4096]{1,0:T(8,128)}), f32[32,4096]{1,0:T(8,128)}) %reduce-scatter.19.cloned.1.call-update) | async-done | bytes 524304 | tf_op jit(solution)/shard_map/reduce_scatter | solution.py:388
  2137.2 361.5 %reduce-scatter.21.cloned.1.call-done = f32[128,1024]{1,0:T(8,128)} async-done(((f32[4096,1024]{1,0:T(8,128)}), f32[128,1024]{1,0:T(8,128)}) %reduce-scatter.21.cloned.1.call-update) | async-done | bytes 524304 | tf_op jit(solution)/shard_map/reduce_scatter | solution.py:390
  (447 shorter events, 592.6 us)
Async XLA Ops:
  7.2 127.1 %all-gather.13.cloned.1.call-start = ((), (), s32[]{:S(2)}) async-start(), calls=%async_computation.16 | async-start | bytes 16896000 | tf_op jit(solution)/shard_map/all_gather | solution.py:187
  7.9 197.2 %all-gather.15.cloned.1.call-start = ((), (), s32[]{:S(2)}) async-start(), calls=%async_computation.17 | async-start | bytes 6488064 | tf_op jit(solution)/shard_map/all_gather | solution.py:191
  8.7 508.8 %all-gather.17.cloned.1.call-start = ((), (), s32[]{:S(2)}) async-start(), calls=%async_computation.18 | async-start | bytes 2162688 | tf_op jit(solution)/shard_map/all_gather | solution.py:192
  9.4 513.3 %all-gather.19.cloned.1.call-start = ((), (), s32[]{:S(2)}) async-start(), calls=%async_computation.19 | async-start | bytes 8650752 | tf_op jit(solution)/shard_map/all_gather | solution.py:195
  58.0 147.2 %copy-start.73 = (f32[1024]{0:T(1024)}, f32[1024]{0:T(1024)S(1)}, u32[]{:S(2)}) copy-start(f32[1024]{0:T(1024)S(1)} %convert_element_type.141) | copy-start | bytes 12292
  58.0 147.2 %copy-start.60 = (f32[1024]{0:T(1024)}, f32[1024]{0:T(1024)S(1)}, u32[]{:S(2)}) copy-start(f32[1024]{0:T(1024)S(1)} %convert_element_type.140) | copy-start | bytes 12292
  58.0 114.9 %copy-start.82 = (s32[256]{0:T(256)}, s32[256]{0:T(256)S(1)}, u32[]{:S(2)}) copy-start(s32[256]{0:T(256)S(1)} %get-tuple-element.506) | copy-start | bytes 3076
  58.0 114.9 %copy-start.84 = (s32[256]{0:T(256)}, s32[256]{0:T(256)S(1)}, u32[]{:S(2)}) copy-start(s32[256]{0:T(256)S(1)} %get-tuple-element.507) | copy-start | bytes 3076
  58.0 114.9 %copy-start.79 = (s32[512]{0:T(512)}, s32[512]{0:T(512)S(1)}, u32[]{:S(2)}) copy-start(s32[512]{0:T(512)S(1)} %multiply_add_fusion.4) | copy-start | bytes 6148
  58.8 114.2 %copy-start.87 = (pred[512]{0:T(512)(128)(4,1)}, pred[512]{0:T(512)(128)(4,1)S(1)}, u32[]{:S(2)}) copy-start(pred[512]{0:T(512)(128)(4,1)S(1)} %get-tuple-element.481) | copy-start | bytes 1540
  132.6 40.4 %copy-start.33 = (bf16[256,1024]{1,0:T(8,128)(2,1)}, bf16[256,1024]{1,0:T(8,128)(2,1)S(1)}, u32[]{:S(2)}) copy-start(bf16[256,1024]{1,0:T(8,128)(2,1)S(1)} %all_gather.65) | copy-start | bytes 1572868
  224.4 22.1 all-to-all-start
  235.9 117.1 %copy-start.56 = (bf16[32,256]{1,0:T(8,128)(2,1)S(1)}, bf16[32,256]{1,0:T(8,128)(2,1)}, u32[]{:S(2)}) copy-start(bf16[32,256]{1,0:T(8,128)(2,1)} %param.41) | copy-start | bytes 49156
  246.5 20.7 all-to-all-start.1
  251.0 299.3 %all-gather.21.cloned.1.call-start = ((), (), s32[]{:S(2)}) async-start(), calls=%async_computation.20 | async-start | bytes 8650752 | tf_op jit(solution)/shard_map/all_gather | solution.py:197
  267.3 170.7 %all-to-all-start.2 = ((bf16[2,2,131072]{2,1,0:T(2,128)(2,1)}), bf16[2,2,131072]{2,1,0:T(2,128)(2,1)}, u32[]{:S(2)}, u32[]{:S(2)}) async-start(bf16[2,2,131072]{2,1,0:T(2,128)(2,1)} %reshape.743), calls=%async_computation.2 | async-start | bytes 2097152 | tf_op jit(solution)/shard_map/all_to_all | solution.py:252
  497.0 15.6 all-to-all-start.3
  501.5 258.7 %reduce-scatter.9.cloned.1.call-start = ((), (), s32[]{:S(2)}) async-start(), calls=%async_computation.21 | async-start | bytes 1572864 | tf_op jit(solution)/shard_map/reduce_scatter | solution.py:323
  567.8 76.7 %copy-start.44 = (f32[2,512]{1,0:T(2,128)S(1)}, f32[2,512]{1,0:T(2,128)}, u32[]{:S(2)}) copy-start(f32[2,512]{1,0:T(2,128)} %fusion.114) | copy-start | bytes 12292
  644.5 115.7 %copy-start.28 = (bf16[1024,256]{1,0:T(8,128)(2,1)S(1)}, bf16[1024,256]{1,0:T(8,128)(2,1)}, u32[]{:S(2)}) copy-start(bf16[1024,256]{1,0:T(8,128)(2,1)} %all_gather.75) | copy-start | bytes 1572868
  644.5 117.2 %copy-start.59 = (f32[32,1,128]{2,1,0:T(1,128)S(1)}, f32[32,1,128]{2,1,0:T(1,128)}, u32[]{:S(2)}) copy-start(f32[32,1,128]{2,1,0:T(1,128)} %convert_element_type.170) | copy-start | bytes 49156
  807.4 18.4 all-to-all-start.4
  950.4 21.2 all-to-all-start.7
  971.6 34.0 %all-to-all-start.6 = ((bf16[2,2,131072]{2,1,0:T(2,128)(2,1)}), bf16[2,2,131072]{2,1,0:T(2,128)(2,1)S(1)}, u32[]{:S(2)}, u32[]{:S(2)}) async-start(bf16[2,2,131072]{2,1,0:T(2,128)(2,1)} %reshape.751), calls=%async_computation.7 | async-start | bytes 2097152 | tf_op jit(solution)/shard_map/all_to_all | solution.py:351
  1005.6 23.9 all-to-all-start.5
  1010.0 195.4 %reduce-scatter.11.cloned.1.call-start = ((), (), s32[]{:S(2)}) async-start(), calls=%async_computation.22 | async-start | bytes 8704000 | tf_op jit(solution)/shard_map/reduce_scatter | solution.py:377
  1097.7 244.6 %reduce-scatter.23.cloned.1.call-start = ((), (), s32[]{:S(2)}) async-start(), calls=%async_computation.28 | async-start | bytes 1081344 | tf_op jit(solution)/shard_map/reduce_scatter | solution.py:391
  1100.7 375.5 %reduce-scatter.13.cloned.1.call-start = ((), (), s32[]{:S(2)}) async-start(), calls=%async_computation.23 | async-start | bytes 1081344 | tf_op jit(solution)/shard_map/reduce_scatter | solution.py:381
  1104.7 512.4 %reduce-scatter.17.cloned.1.call-start = ((), (), s32[]{:S(2)}) async-start(), calls=%async_computation.25 | async-start | bytes 4325376 | tf_op jit(solution)/shard_map/reduce_scatter | solution.py:385
  1108.0 669.9 %reduce-scatter.15.cloned.1.call-start = ((), (), s32[]{:S(2)}) async-start(), calls=%async_computation.24 | async-start | bytes 12976128 | tf_op jit(solution)/shard_map/reduce_scatter | solution.py:384
  1120.1 1017.0 %reduce-scatter.19.cloned.1.call-start = ((), (), s32[]{:S(2)}) async-start(), calls=%async_computation.26 | async-start | bytes 17301504 | tf_op jit(solution)/shard_map/reduce_scatter | solution.py:388
  1133.0 1365.7 %reduce-scatter.21.cloned.1.call-start = ((), (), s32[]{:S(2)}) async-start(), calls=%async_computation.27 | async-start | bytes 17301504 | tf_op jit(solution)/shard_map/reduce_scatter | solution.py:390
  (92 other events, 1328.2 us)
Sparse Core Ops, SparseCore 0:
  10.9 123.3 all-gather.12
  137.2 67.8 all-gather.14
  208.1 58.2 all-gather.16
  269.2 78.7 all-gather.18
  350.8 78.5 all-gather.20
  741.2 18.9 reduce-scatter.8
  1097.8 107.5 reduce-scatter.10
  1208.3 133.9 reduce-scatter.22
  1345.1 131.0 reduce-scatter.12
  1479.0 138.0 reduce-scatter.16
  1624.8 153.1 reduce-scatter.14
  1780.7 356.4 reduce-scatter.18
  2140.0 358.6 reduce-scatter.20
where the time goes:
time: 2520 us; the launch traced here: 2510 us
  waiting for transfers between devices  1370 us (54%)
  matrix products  346 us (14%)
  blocking collectives  337 us (13%)
  other arithmetic  242 us (10%)
  local copies, waits for them, and re-layouts  158 us (6%)
  starting transfers between devices  34.2 us (1%)
    reduce_scatter x1, waiting for transfers between devices, local(): lax.psum_scatter(down_w_grad, ('dp', 'seq'), scatter_dimension=0, tiled=T...  362 us
    reduce_scatter x1, waiting for transfers between devices, local(): lax.psum_scatter(up_w_grad, ('dp', 'seq'), scatter_dimension=0, tiled=True)  359 us
    reduce_scatter x1, waiting for transfers between devices, local(): lax.psum_scatter(qkv_w_grad, ('dp', 'seq'), scatter_dimension=0, tiled=True)  161 us
    reduce_scatter x1, waiting for transfers between devices, local(): lax.psum_scatter(attn_w_grad, ('dp', 'seq'), scatter_dimension=0, tiled=T...  141 us
    reduce_scatter x1, waiting for transfers between devices, local(): lax.psum_scatter(output_w_grad, ('dp', 'seq'), scatter_dimension=0, tiled...  135 us
    reduce_scatter x1, waiting for transfers between devices, local(): lax.psum_scatter(input_w_grad, ('dp', 'seq'), scatter_dimension=0, tiled=...  134 us
    dot_general x10, matrix products, product_right(): lax.dot_general(left, right, (((1,), (1,)), ((), ())), preferred_element_...  102 us
    unnamed x2, blocking collectives  84.2 us
  transfers between devices with their start and end apart: 21, of which 12 were waited for; matrix products, arithmetic and copies ran while one was open for 13% of the time, Pallas kernels for 0%

commit v1 on v0

--- a/solution.py
+++ b/solution.py
@@ -3,11 +3,778 @@
 import jax
 import jax.numpy as jnp
 from jax import lax
+from jax.experimental import pallas as pl
+from jax.experimental.pallas import tpu as pltpu
+from jax.sharding import Mesh
 from jax.sharding import PartitionSpec as P
 
 D = 1024
 HEAD_DIM = 64
 TSTEPS = 1000
+SWAP = ((0, 1), (1, 0))
+BF = jnp.bfloat16
+F32 = jnp.float32
+NEG = -1e30
+MIB = 1 << 20
+
+
+def dot_nn(left, right):
+    return lax.dot_general(left, right, (((1,), (0,)), ((), ())), preferred_element_type=F32)
+
+
+def dot_nt(left, right):
+    return lax.dot_general(left, right, (((1,), (1,)), ((), ())), preferred_element_type=F32)
+
+
+def dot_tn(left, right):
+    return lax.dot_general(left, right, (((0,), (0,)), ((), ())), preferred_element_type=F32)
+
+
+def swap(value, axis):
+    return lax.ppermute(value, axis, SWAP)
+
+
+def ring_down(value, axis):
+    n = lax.axis_size(axis)
+    return lax.ppermute(value, axis, [(i, (i - 1) % n) for i in range(n)])
+
+
+def ring_up(value, axis):
+    n = lax.axis_size(axis)
+    return lax.ppermute(value, axis, [(i, (i + 1) % n) for i in range(n)])
+
+
+def ordered(own, other, place, axis):
+    return jnp.where(
+        place == 0, jnp.stack([own, other], axis), jnp.stack([other, own], axis)
+    )
+
+
+def pick(value, index, axis):
+    return lax.dynamic_index_in_dim(value, index, axis, keepdims=False)
+
+
+def gather_axes(value, order):
+    held = value[None]
+    for axis in order:
+        n = lax.axis_size(axis)
+        parts, moving = [held], held
+        for _ in range(n - 1):
+            moving = swap(moving, axis) if n == 2 else ring_down(moving, axis)
+            parts.append(moving)
+        held = jnp.concatenate(parts, 0)
+    return held
+
+
+def relative_slots(order, targets):
+    flat = 0
+    for axis in reversed(order):
+        n = lax.axis_size(axis)
+        flat = flat * n + (targets[axis] - lax.axis_index(axis)) % n
+    return flat
+
+
+def reduce_axes(value, dims, order):
+    dims = list(dims)
+    last = order[-1]
+    for axis in order:
+        n, here, at = lax.axis_size(axis), lax.axis_index(axis), dims.index(axis)
+        if n == 2:
+            moved = swap(pick(value, 1 - here, at), axis)
+            total = pick(value, here, at).astype(F32) + moved.astype(F32)
+        else:
+            total = pick(value, (here - 1) % n, at)
+            for step in range(1, n):
+                moved = ring_up(total.astype(BF), axis)
+                total = pick(value, (here - 1 - step) % n, at).astype(F32) + moved.astype(F32)
+        value = total if axis == last else total.astype(BF)
+        dims.pop(at)
+    return value
+
+
+def block_copy(slots, blocks, out_shape, out_block, out_map):
+    n, rows, cols = blocks.shape
+
+    def body(slots_ref, in_ref, out_ref):
+        out_ref[...] = in_ref[...].reshape(out_ref.shape)
+
+    return pl.pallas_call(
+        body,
+        out_shape=jax.ShapeDtypeStruct(out_shape, blocks.dtype),
+        grid_spec=pltpu.PrefetchScalarGridSpec(
+            num_scalar_prefetch=1,
+            grid=(n,),
+            in_specs=[pl.BlockSpec((1, rows, cols), lambda i, slots_ref: (slots_ref[i], 0, 0))],
+            out_specs=pl.BlockSpec(out_block, out_map),
+        ),
+        name="block_copy",
+    )(slots, blocks)
+
+
+def attend_body(lo_ref, hi_ref, q_ref, k_ref, v_ref, seg_col_ref, seg_row_ref, o_ref, lse_ref):
+    length = q_ref.shape[0]
+    blk = min(256, length)
+    lane = lax.broadcasted_iota(jnp.int32, (1, 128), 1)
+    masks = (lane < HEAD_DIM, lane >= HEAD_DIM)
+    for qi in range(length // blk):
+        rows = pl.ds(qi * blk, blk)
+        q = q_ref[rows, :]
+        heads = [jnp.where(m, q, jnp.zeros_like(q)) for m in masks]
+        seg_q = seg_col_ref[rows, :]
+
+        def step(kb, carry):
+            at = pl.ds(pl.multiple_of(kb * blk, blk), blk)
+            k, v = k_ref[at, :], v_ref[at, :]
+            same = seg_q == seg_row_ref[:, at]
+            out = []
+            for h in range(2):
+                top, total, acc = carry[h]
+                s = jnp.where(same, dot_nt(heads[h], k), NEG)
+                new_top = jnp.maximum(top, jnp.max(s, axis=1, keepdims=True))
+                keep = jnp.exp(top - new_top)
+                e = jnp.where(same, jnp.exp(s - new_top), 0.0)
+                total = total * keep + jnp.sum(e, axis=1, keepdims=True)
+                acc = acc * keep + dot_nn(e.astype(BF), v)
+                out.append((new_top, total, acc))
+            return tuple(out)
+
+        start = tuple(
+            (
+                jnp.full((blk, 1), NEG, F32),
+                jnp.zeros((blk, 1), F32),
+                jnp.zeros((blk, 128), F32),
+            )
+            for _ in range(2)
+        )
+        done = lax.fori_loop(lo_ref[qi], hi_ref[qi], step, start)
+        outs = [acc / total for _, total, acc in done]
+        o_ref[rows, :] = jnp.where(masks[0], outs[0], outs[1]).astype(BF)
+        lse = [jnp.broadcast_to(top + jnp.log(total), (blk, 128)) for top, total, _ in done]
+        both = jnp.where(masks[0], lse[0], lse[1]).T
+        lse_ref[0, 0:1, rows] = both[0:1, :]
+        lse_ref[0, 1:2, rows] = both[HEAD_DIM : HEAD_DIM + 1, :]
+
+
+def attend(q, k, v, seg_col, seg_row, lo, hi):
+    length, width = q.shape
+    pairs = width // 128
+    spec = pl.BlockSpec((length, 128), lambda i, *_: (0, i))
+    return pl.pallas_call(
+        attend_body,
+        out_shape=(
+            jax.ShapeDtypeStruct((length, width), BF),
+            jax.ShapeDtypeStruct((pairs, 2, length), F32),
+        ),
+        grid_spec=pltpu.PrefetchScalarGridSpec(
+            num_scalar_prefetch=2,
+            grid=(pairs,),
+            in_specs=[
+                spec,
+                spec,
+                spec,
+                pl.BlockSpec((length, 1), lambda i, *_: (0, 0)),
+                pl.BlockSpec((1, length), lambda i, *_: (0, 0)),
+            ],
+            out_specs=(spec, pl.BlockSpec((1, 2, length), lambda i, *_: (i, 0, 0))),
+        ),
+        compiler_params=pltpu.CompilerParams(vmem_limit_bytes=32 * MIB),
+        name="attend",
+    )(lo, hi, q, k, v, seg_col, seg_row)
+
+
+def attend_back_body(
+    lo_ref,
+    hi_ref,
+    q_ref,
+    k_ref,
+    v_ref,
+    o_ref,
+    g_ref,
+    lse_ref,
+    seg_col_ref,
+    seg_row_ref,
+    dq_ref,
+    dk_ref,
+    dv_ref,
+    dk_sum,
+    dv_sum,
+):
+    length = q_ref.shape[0]
+    blk = min(256, length)
+    lane = lax.broadcasted_iota(jnp.int32, (1, 128), 1)
+    masks = (lane < HEAD_DIM, lane >= HEAD_DIM)
+    dk_sum[...] = jnp.zeros_like(dk_sum)
+    dv_sum[...] = jnp.zeros_like(dv_sum)
+    for qi in range(length // blk):
+        rows = pl.ds(qi * blk, blk)
+        q, g = q_ref[rows, :], g_ref[rows, :]
+        zero = jnp.zeros_like(q)
+        q_heads = [jnp.where(m, q, zero) for m in masks]
+        g_heads = [jnp.where(m, g, zero) for m in masks]
+        mixed = (g.astype(F32) * o_ref[rows, :].astype(F32)).T
+        delta = [
+            jnp.sum(mixed[:HEAD_DIM], axis=0, keepdims=True),
+            jnp.sum(mixed[HEAD_DIM:], axis=0, keepdims=True),
+        ]
+        lse = [lse_ref[0, h : h + 1, rows] for h in range(2)]
+        seg_q = seg_row_ref[:, rows]
+
+        def step(kb, dq):
+            at = pl.ds(pl.multiple_of(kb * blk, blk), blk)
+            k, v = k_ref[at, :], v_ref[at, :]
+            same = seg_col_ref[at, :] == seg_q
+            dk, dv = dk_sum[at, :], dv_sum[at, :]
+            for h in range(2):
+                s = dot_nt(k, q_heads[h])
+                p = jnp.where(same, jnp.exp(jnp.where(same, s - lse[h], NEG)), 0.0)
+                dp = dot_nt(v, g_heads[h])
+                ds = (p * (dp - delta[h])).astype(BF)
+                dv = dv + dot_nn(p.astype(BF), g_heads[h])
+                dk = dk + dot_nn(ds, q_heads[h])
+                dq = dq + dot_tn(ds, jnp.where(masks[h], k, jnp.zeros_like(k)))
+            dk_sum[at, :] = dk
+            dv_sum[at, :] = dv
+            return dq
+
+        dq = lax.fori_loop(lo_ref[qi], hi_ref[qi], step, jnp.zeros((blk, 128), F32))
+        dq_ref[rows, :] = dq.astype(BF)
+    dk_ref[...] = dk_sum[...].astype(BF)
+    dv_ref[...] = dv_sum[...].astype(BF)
+
+
+def attend_back(q, k, v, o, g, lse, seg_col, seg_row, lo, hi):
+    length, width = q.shape
+    pairs = width // 128
+    spec = pl.BlockSpec((length, 128), lambda i, *_: (0, i))
+    shape = jax.ShapeDtypeStruct((length, width), BF)
+    return pl.pallas_call(
+        attend_back_body,
+        out_shape=(shape, shape, shape),
+        grid_spec=pltpu.PrefetchScalarGridSpec(
+            num_scalar_prefetch=2,
+            grid=(pairs,),
+            in_specs=[
+                spec,
+                spec,
+                spec,
+                spec,
+                spec,
+                pl.BlockSpec((1, 2, length), lambda i, *_: (i, 0, 0)),
+                pl.BlockSpec((length, 1), lambda i, *_: (0, 0)),
+                pl.BlockSpec((1, length), lambda i, *_: (0, 0)),
+            ],
+            out_specs=(spec, spec, spec),
+            scratch_shapes=[pltpu.VMEM((length, 128), F32), pltpu.VMEM((length, 128), F32)],
+        ),
+        compiler_params=pltpu.CompilerParams(vmem_limit_bytes=32 * MIB),
+        name="attend_back",
+    )(lo, hi, q, k, v, o, g, lse, seg_col, seg_row)
+
+
+def score_body(out_ref, table_ref, raised_ref, tops_ref, ends_ref, acc_ref, scaled, scaled_t):
+    i, j = pl.program_id(0), pl.program_id(1)
+
+    @pl.when(i == 0)
+    def _():
+        rows = table_ref[0].astype(F32)
+        width = rows.shape[1]
+        unit = rows * lax.rsqrt(jnp.mean(rows * rows, axis=1, keepdims=True) + 1e-06)
+        low = (unit * width ** (-0.5)).astype(BF)
+        scaled[j] = low
+        scaled_t[j] = low.astype(F32).T.astype(BF)
+
+    @pl.when(j == 0)
+    def _():
+        ends_ref[...] = jnp.full_like(ends_ref, NEG)
+        acc_ref[...] = jnp.zeros_like(acc_ref)
+
+    logits = dot_nt(scaled[j], out_ref[...])
+    top = ends_ref[0:1, :]
+    total = jnp.where(j == 0, 0.0, ends_ref[1:2, :])
+    new_top = jnp.maximum(top, jnp.max(logits, axis=0, keepdims=True))
+    keep = jnp.exp(top - new_top)
+    e = jnp.exp(logits - new_top)
+    low = e.astype(BF)
+    raised_ref[0] = low
+    ends_ref[0:1, :] = new_top
+    ends_ref[1:2, :] = total * keep + jnp.sum(e, axis=0, keepdims=True)
+    acc_ref[...] = acc_ref[...] * keep + dot_nn(scaled_t[j], low)
+    tops_ref[0] = new_top
+
+
+def score(outputs, table):
+    tokens, width = outputs.shape
+    blocks, rows, _ = table.shape
+    tile = math.gcd(tokens, 512)
+    return pl.pallas_call(
+        score_body,
+        out_shape=(
+            jax.ShapeDtypeStruct((blocks, rows, tokens), BF),
+            jax.ShapeDtypeStruct((blocks, 1, tokens), F32),
+            jax.ShapeDtypeStruct((8, tokens), F32),
+            jax.ShapeDtypeStruct((width, tokens), F32),
+        ),
+        grid=(tokens // tile, blocks),
+        in_specs=[
+            pl.BlockSpec((tile, width), lambda i, j: (i, 0)),
+            pl.BlockSpec(
+                (1, rows, width), lambda i, j: (jnp.where(i == 0, j, blocks - 1), 0, 0)
+            ),
+        ],
+        out_specs=(
+            pl.BlockSpec((1, rows, tile), lambda i, j: (j, 0, i)),
+            pl.BlockSpec((1, 1, tile), lambda i, j: (j, 0, i)),
+            pl.BlockSpec((8, tile), lambda i, j: (0, i)),
+            pl.BlockSpec((width, tile), lambda i, j: (0, i)),
+        ),
+        scratch_shapes=[
+            pltpu.VMEM((blocks, rows, width), BF),
+            pltpu.VMEM((blocks, width, rows), BF),
+        ],
+        compiler_params=pltpu.CompilerParams(vmem_limit_bytes=48 * MIB),
+        name="score",
+    )(outputs, table)
+
+
+def table_product_body(raised_ref, out_ref, coef_ref, sum_ref):
+    j = pl.program_id(0)
+    lane = lax.broadcasted_iota(jnp.int32, coef_ref.shape, 1)
+    coef = jnp.sum(jnp.where(lane == j, coef_ref[...], 0.0), axis=1, keepdims=True)
+    weighted = (out_ref[...].astype(F32) * coef).astype(BF)
+    sum_ref[0] = dot_nn(raised_ref[0], weighted)
+
+
+def table_product(raised, outputs, coef):
+    blocks, rows, tokens = raised.shape
+    width = outputs.shape[1]
+    return pl.pallas_call(
+        table_product_body,
+        out_shape=jax.ShapeDtypeStruct((blocks, rows, width), F32),
+        grid=(blocks,),
+        in_specs=[
+            pl.BlockSpec((1, rows, tokens), lambda j: (j, 0, 0)),
+            pl.BlockSpec((tokens, width), lambda j: (0, 0)),
+            pl.BlockSpec((tokens, blocks), lambda j: (0, 0)),
+        ],
+        out_specs=pl.BlockSpec((1, rows, width), lambda j: (j, 0, 0)),
+        compiler_params=pltpu.CompilerParams(vmem_limit_bytes=48 * MIB),
+        name="table_product",
+    )(raised, outputs, coef)
+
+
+def table_add_body(sum_ref, slot_ref, grad_ref, out_ref):
+    j = pl.program_id(0)
+    rows = sum_ref.shape[1]
+    row = lax.broadcasted_iota(jnp.int32, (rows, 1), 0) + j * rows
+    chosen = (row == slot_ref[...]).astype(F32).astype(BF)
+    out_ref[0] = (sum_ref[0] + dot_nn(chosen, grad_ref[...])).astype(BF)
+
+
+def table_add(sums, slots, grads):
+    blocks, rows, width = sums.shape
+    tokens = grads.shape[0]
+    return pl.pallas_call(
+        table_add_body,
+        out_shape=jax.ShapeDtypeStruct(sums.shape, BF),
+        grid=(blocks,),
+        in_specs=[
+            pl.BlockSpec((1, rows, width), lambda j: (j, 0, 0)),
+            pl.BlockSpec((1, tokens), lambda j: (0, 0)),
+            pl.BlockSpec((tokens, width), lambda j: (0, 0)),
+        ],
+        out_specs=pl.BlockSpec((1, rows, width), lambda j: (j, 0, 0)),
+        compiler_params=pltpu.CompilerParams(vmem_limit_bytes=48 * MIB),
+        name="table_add",
+    )(sums, slots, grads)
+
+
+def norm_parts(hidden):
+    centre = hidden - jnp.mean(hidden, axis=-1, keepdims=True)
+    spread = jnp.mean(centre * centre, axis=-1, keepdims=True)
+    inverse = lax.rsqrt(spread + 1e-05)
+    return centre * inverse, inverse
+
+
+def norm_back(grad, gain, normed, inverse):
+    grad_normed = grad * gain
+    first = jnp.mean(grad_normed, axis=-1, keepdims=True)
+    second = jnp.mean(grad_normed * normed, axis=-1, keepdims=True)
+    return inverse * (grad_normed - first - normed * second)
+
+
+def noise_field(row_seed, length, channel_count):
+    position = lax.iota(jnp.int32, length)[:, None]
+    channel = lax.iota(jnp.int32, channel_count)[None, :]
+    mixed_once = (row_seed + 7919 * position + 104729 * channel) % 65521
+    mixed_twice = (mixed_once * (mixed_once % 32719) + 31 * channel) % 65521
+    return (mixed_twice.astype(F32) / 32760.5 - 1.0) * 1.7320508
+
+
+def paired(
+    token_ids,
+    segment_ids,
+    time_steps,
+    row_seeds,
+    loss_weights,
+    embed_table,
+    input_proj,
+    attn_gain,
+    attn_bias,
+    qkv_proj,
+    attn_proj,
+    mlp_gain,
+    mlp_bias,
+    up_proj,
+    up_bias,
+    down_proj,
+    output_proj,
+):
+    z, y, c, x = (lax.axis_index(a) for a in ("z", "y", "c", "x"))
+    groups = lax.axis_size("z") * lax.axis_size("y")
+    length = token_ids.shape[1]
+    half = length // 2
+    block_len, width = embed_table.shape
+    ff = up_proj.shape[1]
+    rows_here = qkv_proj.shape[0]
+    heads = D // HEAD_DIM
+    ff_block = down_proj.shape[0] * 2
+
+    cut = block_len // 32 * 16
+    table_a = gather_axes(embed_table[:cut], ("z", "y"))
+    table_b = gather_axes(embed_table[cut:], ("y", "z"))
+
+    meta = jnp.concatenate([token_ids[0], segment_ids[0], time_steps, row_seeds])
+    meta_two = ordered(meta, swap(meta, "c"), c, 0)
+    weight_c = ordered(loss_weights[0], swap(loss_weights[0], "c"), c, 0)
+    weight_two = ordered(weight_c, swap(weight_c, "x"), x, 1).reshape(2, length)
+    ids_two = meta_two[:, :length]
+    own_meta = pick(meta_two, x, 0)
+    segments = own_meta[length : 2 * length]
+    weight_row = pick(weight_two, x, 0)
+    fraction = own_meta[2 * length].astype(F32) / (TSTEPS - 1)
+    noise_level = 0.3 * jnp.exp(fraction * math.log(30.0))
+    input_scale = lax.rsqrt(1.0 + noise_level * noise_level)
+    residual_scale = 0.5 + fraction
+    noise = noise_field(own_meta[2 * length + 1], length, width)
+
+    small = jnp.concatenate(
+        [
+            input_proj.reshape(-1, width),
+            output_proj,
+            jnp.concatenate([attn_gain, attn_bias, mlp_gain, mlp_bias, up_bias]).reshape(1, width),
+            jnp.zeros((15, width), BF),
+        ]
+    )
+    small_pair = ordered(small, swap(small, "c"), c, 0)
+    small_rows = small.shape[0]
+    small_all = gather_axes(small_pair.reshape(2 * small_rows, width), ("z", "y", "x"))
+
+    qkv_split = qkv_proj.reshape(rows_here, 3, heads // 2, 2, HEAD_DIM)
+    qkv_pair = ordered(
+        pick(qkv_split, c, 3).reshape(rows_here, -1),
+        swap(pick(qkv_split, 1 - c, 3).reshape(rows_here, -1), "c"),
+        c,
+        0,
+    ).reshape(2 * rows_here, 3 * D // 2)
+    up_split = up_proj.reshape(rows_here, groups, 2, ff_block)
+    up_pair = ordered(
+        pick(up_split, c, 2).reshape(rows_here, -1),
+        swap(pick(up_split, 1 - c, 2).reshape(rows_here, -1), "c"),
+        c,
+        0,
+    ).reshape(2 * rows_here, ff // 2)
+
+    block = jnp.arange(2 * groups, dtype=jnp.int32)
+    place = {"z": block // 4, "y": block // 2 % 2, "x": block % 2}
+
+    def gathered_rows(shard, order):
+        held = gather_axes(shard, order)
+        n, rows, cols = held.shape
+        return block_copy(
+            relative_slots(order, place),
+            held,
+            (n, rows, cols),
+            (1, rows, cols),
+            lambda i, slots_ref: (i, 0, 0),
+        ).reshape(n * rows, cols)
+
+    def gathered_pairs(shard, order):
+        held = gather_axes(shard, order)
+        n, rows, cols = held.shape
+        return block_copy(
+            relative_slots(order, place),
+            held,
+            (groups, 2, 2, rows // 2, cols),
+            (1, 2, 1, rows // 2, cols),
+            lambda i, slots_ref: (i // 2, 0, i % 2, 0, 0),
+        ).reshape(n * rows, cols)
+
+    small_full = block_copy(
+        relative_slots(("z", "y", "x"), place),
+        small_all,
+        small_all.shape,
+        (1,) + small_all.shape[1:],
+        lambda i, slots_ref: (i, 0, 0),
+    ).reshape(groups, 2, 2, small_rows, width)
+    small_full = small_full.transpose(0, 2, 1, 3, 4)
+    input_count = input_proj.shape[0] * D // width
+    input_full = small_full[..., :input_count, :].reshape(width, D)
+    output_full = small_full[..., input_count : input_count + rows_here, :].reshape(D, width)
+    vectors = small_full[..., input_count + rows_here, :]
+    gain_one, bias_one, gain_two, bias_two = (
+        vectors[..., k * rows_here : (k + 1) * rows_here].reshape(1, D).astype(F32)
+        for k in range(4)
+    )
+    up_bias_half = pick(vectors[..., 4 * rows_here :], c, 1).reshape(1, ff // 2).astype(F32)
+
+    qkv_half = gathered_pairs(qkv_pair, ("z", "y", "x"))
+    attn_half = gathered_rows(attn_proj, ("z", "x", "y"))
+    up_half = gathered_pairs(up_pair, ("z", "x", "y"))
+    down_half = gathered_rows(down_proj, ("z", "y", "x"))
+
+    flat_ids = ids_two.reshape(-1)
+    owner = flat_ids // block_len
+    within = flat_ids % block_len
+    home = {"z": owner // 8, "y": owner // 4 % 2}
+    mine = owner % 4 == c * 2 + x
+    table_rows = jnp.concatenate(
+        [
+            table_a,
+            table_b.reshape(2 * groups // 4, 2, block_len - cut, width)
+            .transpose(1, 0, 2, 3)
+            .reshape(groups, block_len - cut, width),
+        ],
+        axis=1,
+    )
+    slot = relative_slots(("z", "y"), home) * block_len + within
+    found = jnp.take(
+        table_rows.reshape(groups * block_len, width), jnp.where(mine, slot, 0), axis=0
+    )
+    found = jnp.where(mine[:, None], found, jnp.zeros_like(found)).reshape(2, length, width)
+
+    def to_rows(terms, kind):
+        split = terms.reshape(2, 2, half, width)
+        moved = swap(pick(split, 1 - c, 1).astype(kind), "c")
+        both = pick(split, c, 1).astype(F32) + moved.astype(F32)
+        moved = swap(pick(both, 1 - x, 0).astype(kind), "x")
+        own = (pick(both, x, 0).astype(F32) + moved.astype(F32)).astype(kind)
+        return ordered(own, swap(own, "c"), c, 0).reshape(length, width)
+
+    def to_pair(row):
+        own = pick(row.reshape(2, half, width), c, 0)
+        moved = swap(own, "x")
+        other = ordered(moved, swap(moved, "c"), c, 0).reshape(length, width)
+        return ordered(row, other, x, 0)
+
+    raw = to_rows(found, BF).astype(F32)
+    unit = raw * lax.rsqrt(jnp.mean(raw * raw, axis=1, keepdims=True) + 1e-06)
+    target = (unit * width ** (-0.5)).astype(BF)
+    inputs = (input_scale * (unit + noise_level * noise)).astype(BF)
+
+    hidden_zero = dot_nn(inputs, input_full)
+    normed_one, inverse_one = norm_parts(hidden_zero)
+    first_in = (normed_one * gain_one + bias_one).astype(BF)
+    qkv = dot_nn(first_in, qkv_half)
+    split = D // 2
+    queries = (qkv[:, :split] * HEAD_DIM ** (-0.5)).astype(BF)
+    keys = qkv[:, split : 2 * split].astype(BF)
+    values = qkv[:, 2 * split :].astype(BF)
+    seg_col, seg_row = segments[:, None], segments[None, :]
+    blk = min(256, length)
+    edges = segments.reshape(length // blk, blk)
+    before = jnp.sum(seg_row < edges[:, :1], axis=1, dtype=jnp.int32)
+    through = jnp.sum(seg_row <= edges[:, -1:], axis=1, dtype=jnp.int32)
+    low_block, high_block = before // blk, (through + blk - 1) // blk
+    attended, log_total = attend(queries, keys, values, seg_col, seg_row, low_block, high_block)
+
+    def both_cores(part):
+        return part + swap(part.astype(BF), "c").astype(F32)
+
+    hidden_one = hidden_zero + residual_scale * both_cores(dot_nn(attended, attn_half))
+    normed_two, inverse_two = norm_parts(hidden_one)
+    second_in = (normed_two * gain_two + bias_two).astype(BF)
+    pre_act = dot_nn(second_in, up_half) + up_bias_half
+    below = 0.5 * (1.0 + lax.erf(pre_act * math.sqrt(0.5)))
+    activated = (pre_act * below).astype(BF)
+    slope = (
+        below + pre_act * (jnp.exp(-0.5 * pre_act * pre_act) * (1.0 / math.sqrt(2.0 * math.pi)))
+    ).astype(BF)
+    hidden_two = hidden_one + residual_scale * both_cores(dot_nn(activated, down_half))
+    final_in = hidden_two.astype(BF)
+    outputs = dot_nn(final_in, output_full).astype(BF)
+
+    outputs_two = to_pair(outputs).reshape(2 * length, width)
+    raised, tops, ends, reached = score(outputs_two, table_rows)
+    ends = ends[:2]
+
+    def joined(first, second):
+        top = jnp.maximum(first[0], second[0])
+        return jnp.stack(
+            [top, first[1] * jnp.exp(first[0] - top) + second[1] * jnp.exp(second[0] - top)]
+        )
+
+    all_ends = joined(ends, swap(ends, "c"))
+    all_ends = joined(all_ends, swap(all_ends, "x"))
+    log_sum = all_ends[0] + jnp.log(all_ends[1])
+    share = (reached * jnp.exp(ends[0] - log_sum)[None, :]).T
+    expected = to_rows(share.reshape(2, length, width), BF).astype(F32)
+    log_row = pick(log_sum.reshape(2, length), x, 0)
+    chosen = jnp.sum(outputs.astype(F32) * target.astype(F32), axis=1)
+    loss_row = log_row - chosen
+    loss_two = ordered(loss_row, swap(loss_row, "x"), x, 0)
+    token_loss = pick(pick(loss_two, c, 0).reshape(2, half), x, 0)[None]
+
+    out_grad = (weight_row[:, None] * (expected - target.astype(F32))).astype(BF)
+    coef = (
+        (weight_two.reshape(-1) * width ** (-0.5))[None, :] * jnp.exp(tops[:, 0] - log_sum[None, :])
+    ).T
+    table_sums = table_product(raised, outputs_two, coef)
+
+    xyz, yxz = ("x", "y", "z"), ("y", "x", "z")
+    row_dims = ("z", "y", "x", None, None)
+    pair_dims = ("z", "y", None, "x", None, None)
+    zy = (lax.axis_size("z"), lax.axis_size("y"))
+
+    def reduced_rows(grad, order):
+        rows = grad.shape[0] // (2 * groups)
+        shaped = grad.astype(BF).reshape(zy + (2, rows, grad.shape[1]))
+        return reduce_axes(shaped, row_dims, order)
+
+    def reduced_pairs(grad, order):
+        rows = grad.shape[0] // (4 * groups)
+        shaped = grad.astype(BF).reshape(zy + (2, 2, rows, grad.shape[1]))
+        return reduce_axes(shaped, pair_dims, order)
+
+    output_w_grad = dot_tn(final_in, out_grad)
+    hidden_two_grad = dot_nt(out_grad, output_full)
+    branch_grad = (residual_scale * hidden_two_grad).astype(BF)
+    down_own = reduced_rows(dot_tn(activated, branch_grad), xyz)
+    pre_grad = (dot_nt(branch_grad, down_half) * slope.astype(F32)).astype(BF)
+    up_sum = reduced_pairs(dot_tn(second_in, pre_grad), yxz)
+    up_bias_part = jnp.sum(pre_grad, axis=0, dtype=F32)
+    second_grad = both_cores(dot_nt(pre_grad, up_half))
+    gain_two_part = jnp.sum(second_grad * normed_two, axis=0)
+    bias_two_part = jnp.sum(second_grad, axis=0)
+    hidden_one_grad = hidden_two_grad + norm_back(second_grad, gain_two, normed_two, inverse_two)
+    attn_grad = (residual_scale * hidden_one_grad).astype(BF)
+    attn_own = reduced_rows(dot_tn(attended, attn_grad), yxz)
+    attended_grad = dot_nt(attn_grad, attn_half).astype(BF)
+    query_grad, key_grad, value_grad = attend_back(
+        queries,
+        keys,
+        values,
+        attended,
+        attended_grad,
+        log_total,
+        seg_col,
+        seg_row,
+        low_block,
+        high_block,
+    )
+    qkv_grad = jnp.concatenate(
+        [query_grad * jnp.asarray(HEAD_DIM ** (-0.5), BF), key_grad, value_grad], axis=1
+    )
+    qkv_sum = reduced_pairs(dot_tn(first_in, qkv_grad), xyz)
+    first_grad = both_cores(dot_nt(qkv_grad, qkv_half))
+    gain_one_part = jnp.sum(first_grad * normed_one, axis=0)
+    bias_one_part = jnp.sum(first_grad, axis=0)
+    hidden_zero_grad = (
+        hidden_one_grad + norm_back(first_grad, gain_one, normed_one, inverse_one)
+    ).astype(BF)
+    input_w_grad = dot_tn(inputs, hidden_zero_grad)
+    embed_grad = input_scale * dot_nt(hidden_zero_grad, input_full)
+    token_grad = (
+        embed_grad - (weight_row * width ** (-0.5))[:, None] * outputs.astype(F32)
+    ).astype(BF)
+
+    token_grad_two = to_pair(token_grad).reshape(2 * length, width)
+    slots_here = jnp.where(mine, slot, -1)[None, :]
+    table_terms = table_add(table_sums, slots_here, token_grad_two)
+    relative = (2, zy[0], block_len, width)
+
+    def reduced_table(terms, order):
+        for axis in order:
+            at = 0 if axis == "y" or terms.ndim == 3 else 1
+            n = lax.axis_size(axis)
+            if n == 2:
+                keep, send = jnp.take(terms, 0, at), jnp.take(terms, 1, at)
+                terms = keep.astype(F32) + swap(send, axis).astype(F32)
+            else:
+                total = jnp.take(terms, n - 1, at)
+                for k in range(n - 2, -1, -1):
+                    total = jnp.take(terms, k, at).astype(F32) + ring_down_from(
+                        total.astype(BF), axis
+                    ).astype(F32)
+                terms = total
+            if axis != order[-1]:
+                terms = terms.astype(BF)
+        return terms
+
+    def ring_down_from(value, axis):
+        return ring_up(value, axis)
+
+    shaped = table_terms.reshape(relative)
+    unit_grad = jnp.concatenate(
+        [
+            reduced_table(shaped[:, :, :cut], ("y", "z")),
+            reduced_table(shaped[:, :, cut:], ("z", "y")),
+        ],
+        axis=0,
+    )
+    own_rows = embed_table.astype(F32)
+    inverse = lax.rsqrt(jnp.mean(own_rows * own_rows, axis=1, keepdims=True) + 1e-06)
+    along = jnp.mean(own_rows * unit_grad, axis=1, keepdims=True)
+    table_grad = inverse * unit_grad - own_rows * (inverse * inverse * inverse * along)
+
+    input_rows = input_proj.shape[0]
+    small_grad = jnp.concatenate(
+        [
+            pick(input_w_grad.reshape(zy + (2, 2, input_rows, D)), c, 2).reshape(
+                zy + (2, -1, width)
+            ),
+            pick(output_w_grad.reshape(zy + (2, 2, rows_here, width)), c, 2),
+            jnp.concatenate(
+                [
+                    pick(part.reshape(zy + (2, 2, rows_here)), c, 2)
+                    for part in (gain_one_part, bias_one_part, gain_two_part, bias_two_part)
+                ]
+                + [up_bias_part.reshape(zy + (2, -1))],
+                axis=-1,
+            )[..., None, :],
+            jnp.zeros(zy + (2, 15, width), F32),
+        ],
+        axis=-2,
+    )
+    small_own = reduce_axes(small_grad.astype(BF), row_dims, xyz)
+    input_own = small_own[:input_count].reshape(input_rows, D)
+    output_own = small_own[input_count : input_count + rows_here]
+    vector_own = small_own[input_count + rows_here]
+    gains = [vector_own[k * rows_here : (k + 1) * rows_here] for k in range(4)]
+
+    def columns_back(sums, split_shape, axis):
+        mine_rows, other_rows = pick(sums, c, 0), pick(sums, 1 - c, 0)
+        other_cols = swap(other_rows, "c")
+        return ordered(
+            mine_rows.reshape(split_shape), other_cols.reshape(split_shape), c, axis
+        ).reshape(rows_here, -1)
+
+    qkv_own = columns_back(qkv_sum, (rows_here, 3 * heads // 2, HEAD_DIM), 2)
+    up_own = columns_back(up_sum, (rows_here, groups, ff_block), 2)
+    return (
+        token_loss,
+        table_grad,
+        input_own,
+        gains[0],
+        gains[1],
+        qkv_own,
+        attn_own,
+        gains[2],
+        gains[3],
+        up_own,
+        vector_own[4 * rows_here :],
+        down_own,
+        output_own,
+    )
 
 
 def combined_all(shard, axis, combine):
@@ -50,7 +817,7 @@
     return jax.nn.gelu(pre_act, approximate=False)
 
 
-def noise_field(row_seeds, positions, channel_count):
+def noise_rows(row_seeds, positions, channel_count):
     channel = lax.iota(jnp.int32, channel_count)
     mixed_once = (
         row_seeds[:, None, None] + 7919 * positions[None, :, None] + 104729 * channel[None, None, :]
@@ -226,7 +993,7 @@
         local_rows // block_len * seq_count + seq_place
     ) * block_len + local_rows % block_len
     noise_level, input_scale, residual_scale = time_terms(time_steps)
-    noise = noise_field(row_seeds, positions, embed_width)
+    noise = noise_rows(row_seeds, positions, embed_width)
     embedded = jnp.take(unit, own_ids, axis=0)
     inputs = (
         (input_scale[:, None, None] * (embedded + noise_level[:, None, None] * noise))
@@ -394,38 +1161,45 @@
 
 
 def solution(mesh):
+    dp, seq = mesh.shape["dp"], mesh.shape["seq"]
+    if (dp, seq) == (16, 2):
+        inner = Mesh(mesh.devices.reshape(dp // 4, 2, 2, seq), ("z", "y", "c", "x"))
+        dp_names, seq_names, body = ("z", "y", "c"), ("x",), paired
+    else:
+        inner, dp_names, seq_names, body = mesh, ("dp",), ("seq",), local
+    every = dp_names + seq_names
     in_specs = (
-        P("dp", None),
-        P("dp", None),
-        P("dp"),
-        P("dp"),
-        P("dp", "seq"),
-        P(("dp", "seq"), None),
-        P(("dp", "seq"), None),
-        P(("dp", "seq")),
-        P(("dp", "seq")),
-        P(("dp", "seq"), None),
-        P(("dp", "seq"), None),
-        P(("dp", "seq")),
-        P(("dp", "seq")),
-        P(("dp", "seq"), None),
-        P(("dp", "seq")),
-        P(("dp", "seq"), None),
-        P(("dp", "seq"), None),
+        P(dp_names, None),
+        P(dp_names, None),
+        P(dp_names),
+        P(dp_names),
+        P(dp_names, seq_names),
+        P(every, None),
+        P(every, None),
+        P(every),
+        P(every),
+        P(every, None),
+        P(every, None),
+        P(every),
+        P(every),
+        P(every, None),
+        P(every),
+        P(every, None),
+        P(every, None),
     )
     out_specs = (
-        P("dp", "seq"),
-        P(("dp", "seq"), None),
-        P(("dp", "seq"), None),
-        P(("dp", "seq")),
-        P(("dp", "seq")),
-        P(("dp", "seq"), None),
-        P(("dp", "seq"), None),
-        P(("dp", "seq")),
-        P(("dp", "seq")),
-        P(("dp", "seq"), None),
-        P(("dp", "seq")),
-        P(("dp", "seq"), None),
-        P(("dp", "seq"), None),
-    )
-    return jax.shard_map(local, mesh=mesh, in_specs=in_specs, out_specs=out_specs, check_vma=False)
+        P(dp_names, seq_names),
+        P(every, None),
+        P(every, None),
+        P(every),
+        P(every),
+        P(every, None),
+        P(every, None),
+        P(every),
+        P(every),
+        P(every, None),
+        P(every),
+        P(every, None),
+        P(every, None),
+    )
+    return jax.shard_map(body, mesh=inner, in_specs=in_specs, out_specs=out_specs, check_vma=False)

time: 2520 us -> 843 us (0.33)
  waiting for transfers between devices: 1370 us -> 206 us
  blocking collectives: 337 us -> 0 us
  matrix products: 346 us -> 79.4 us
  Pallas kernels: 0 us -> 225 us
  other arithmetic: 242 us -> 91.2 us
  starting transfers between devices: 34.2 us -> 79.8 us
    reduce_scatter x8 -> x0, waiting for transfers between devices: 1320 us -> none  [the longest x1 362 us: local(): lax.psum_scatter(down_w_grad, ('dp', 'seq'), scatter_dimension=0, tiled=T...]
    dot_general x40 -> x18, matrix products: 346 us -> 79.4 us  [the longest x6 30 us: dot_nn(): lax.dot_general(left, right, (((1,), (0,)), ((), ())), preferred_element_...]
    all_gather x9 -> x0, blocking collectives: 253 us -> none  [the longest x1 74.4 us: local(): lax.all_gather(output_proj, ('dp', 'seq'), axis=0, tiled=True)]
    pallas_call x0 -> x10, Pallas kernels: none -> 225 us  [the longest x5 60.2 us: block_copy(): pl.pallas_call(body, out_shape=jax.ShapeDtypeStruct(out_shape, blocks.dty...]
    ppermute x0 -> x91, waiting for transfers between devices: none -> 206 us  [the longest x49 94.7 us: swap(): return lax.ppermute(value, axis, SWAP)]
    unnamed x2 -> x0, blocking collectives: 84.2 us -> none
    ppermute x0 -> x91, starting transfers between devices: none -> 79.8 us  [the longest x21 44.5 us: ring_down(): return lax.ppermute(value, axis, [(i, (i - 1) % n) for i in range(n)])]
    unnamed x14 -> x2, other arithmetic: 63.9 us -> 0.03 us
  transfers between devices with their start and end apart: 21 -> 91, of which waited for: 12 -> 40; matrix products, arithmetic and copies ran while one was open for 13% -> 28% of each run, Pallas kernels for 0% -> 27%
where the time goes in v1:
time: 843 us; the launch traced here: 830 us
  Pallas kernels  225 us (27%)
  waiting for transfers between devices  206 us (24%)
  local copies, waits for them, and re-layouts  143 us (17%)
  other arithmetic  91.2 us (11%)
  starting transfers between devices  79.8 us (9%)
  matrix products  79.4 us (9%)
    ppermute x49, waiting for transfers between devices, swap(): return lax.ppermute(value, axis, SWAP)  94.7 us
    ppermute x21, waiting for transfers between devices, ring_up(): return lax.ppermute(value, axis, [(i, (i + 1) % n) for i in range(n)])  79.9 us
    pallas_call x5, Pallas kernels, block_copy(): pl.pallas_call(body, out_shape=jax.ShapeDtypeStruct(out_shape, blocks.dty...  60.2 us
    pallas_call x1, Pallas kernels, score(): pl.pallas_call(score_body, out_shape=(jax.ShapeDtypeStruct((blocks, rows,...  47.6 us
    unnamed x177, local copies, waits for them, and re-layouts  45.4 us
    pallas_call x1, Pallas kernels, attend(): pl.pallas_call(attend_body, out_shape=(jax.ShapeDtypeStruct((length, widt...  44.6 us
    ppermute x21, starting transfers between devices, ring_down(): return lax.ppermute(value, axis, [(i, (i - 1) % n) for i in range(n)])  44.5 us
    pallas_call x1, Pallas kernels, attend_back(): pl.pallas_call(attend_back_body, out_shape=(shape, shape, shape), grid_sp...  42.5 us
  transfers between devices with their start and end apart: 91, of which 40 were waited for; matrix products, arithmetic and copies ran while one was open for 28% of the time, Pallas kernels for 27%

profile of v1, /device:TPU:0, one launch (start us, length us, event | category | flops | bytes accessed | tf_op | source)
XLA Modules:
  0.0 829.7 jit_solution(3356704964327835093)
XLA Ops:
  86.2 16.0 %collective-permute-done.20 = bf16[1,64,1536]{2,1,0:T(8,128)(2,1)S(1)} collective-permute-done((bf16[1,64,1536]{2,1,0:T(8,128)(2,1)S(1)}, bf16[1,64,1536]{2,1,0:T(8,128)(2,1)S(1)}, u32[]{:S(2)}, u32[]{:S(2)}) %collective-permute-start.20) | collective-permute-done | bytes 196640 | tf_op jit(solution)/shard_map/ppermute | solution.py:39
  146.3 9.5 %block_copy.7 = bf16[16,32,1024]{2,1,0:T(8,128)(2,1)} custom-call(s32[16]{0:T(128)} %multiply_add_fusion.5.slots_ref, bf16[16,32,1024]{2,1,0:T(8,128)(2,1)} %constant_dynamic-update-slice_fusion.37.in_ref), custom_call_target="tpu_custom_call" | custom-call | tf_op jit(solution)/shard_map/block_copy/pallas_call | solution.py:101
  158.2 9.8 %block_copy.5 = bf16[16,160,256]{2,1,0:T(8,128)(2,1)} custom-call(s32[16]{0:T(128)} %multiply_add_fusion.6.slots_ref, bf16[16,160,256]{2,1,0:T(8,128)(2,1)} %constant_dynamic-update-slice_fusion.15.in_ref), custom_call_target="tpu_custom_call" | custom-call | tf_op jit(solution)/shard_map/block_copy/pallas_call | solution.py:101
  178.6 9.3 %gather_fusion = bf16[2048,256]{1,0:T(8,128)(2,1)S(1)} fusion(bf16[8000,256]{1,0:T(8,128)(2,1)} %bitcast.416, s32[2048]{0:T(1024)S(1)} %broadcast_clamp_fusion), kind=kCustom, calls=%fused_computation | custom fusion | bytes 2105344 | tf_op jit(solution)/shard_map/jit(_take)/gather | solution.py:550
  210.5 24.2 %collective-permute-done.23 = bf16[8,64,1536]{2,1,0:T(8,128)(2,1)S(1)} collective-permute-done((bf16[8,64,1536]{2,1,0:T(8,128)(2,1)}, bf16[8,64,1536]{2,1,0:T(8,128)(2,1)S(1)}, u32[]{:S(2)}, u32[]{:S(2)}) %collective-permute-start.23) | collective-permute-done | bytes 1572896 | tf_op jit(solution)/shard_map/ppermute | solution.py:34
  236.0 10.6 %block_copy.6 = bf16[8,2,2,32,1536]{4,3,2,1,0:T(8,128)(2,1)} custom-call(s32[16]{0:T(128)} %multiply_add_fusion.6.slots_ref, bf16[16,64,1536]{2,1,0:T(8,128)(2,1)} %constant_dynamic-update-slice_fusion.26.in_ref), custom_call_target="tpu_custom_call" | custom-call | tf_op jit(solution)/shard_map/block_copy/pallas_call | solution.py:101
  246.7 6.5 fusion.153
  254.2 44.6 %attend.1 = (bf16[1024,512]{1,0:T(8,128)(2,1)S(1)}, f32[4,2,1024]{2,1,0:T(2,128)S(1)}) custom-call(s32[4]{0:T(128)S(1)} %get-tuple-element.326.lo_ref, s32[4]{0:T(128)S(1)} %get-tuple-element.325.hi_ref, bf16[1024,512]{1,0:T(8,128)(2,1)S(1)} %fusion.8.q_ref, bf16[1024,512]{1,0:T(8,128)(2,1)S(1)} %get-tuple-element.216.k_ref, ...), custom_call_target="tpu_custom_call" | custom-call | tf_op jit(solution)/shard_map/attend/pallas_call | solution.py:162
  306.1 10.8 %block_copy.9 = bf16[16,128,1024]{2,1,0:T(8,128)(2,1)} custom-call(s32[16]{0:T(128)} %multiply_add_fusion.6.slots_ref, bf16[16,128,1024]{2,1,0:T(8,128)(2,1)} %constant_dynamic-update-slice_fusion.59.in_ref), custom_call_target="tpu_custom_call" | custom-call | tf_op jit(solution)/shard_map/block_copy/pallas_call | solution.py:101
  320.1 19.4 %block_copy.8 = bf16[8,2,2,32,2048]{4,3,2,1,0:T(8,128)(2,1)} custom-call(s32[16]{0:T(128)} %multiply_add_fusion.5.slots_ref, bf16[16,64,2048]{2,1,0:T(8,128)(2,1)} %constant_dynamic-update-slice_fusion.48.in_ref), custom_call_target="tpu_custom_call" | custom-call | tf_op jit(solution)/shard_map/block_copy/pallas_call | solution.py:101
  348.5 9.4 %multiply_convert_fusion.1 = (bf16[1024,2048]{1,0:T(8,128)(2,1)S(1)}, f32[1024,2048]{1,0:T(8,128)}) fusion(f32[2048]{0:T(1024)S(1)} %bitcast.499, bf16[1024,2048]{1,0:T(8,128)(2,1)S(1)} %bitcast.423, f32[1024,1024]{0,1:T(8,128)S(1)} %get-tuple-element.208, f32[1024]{0:T(1024)S(1)} %reshape.1697, f32[1024]{0:T(1024)S(1)} %reshape.1696, ...), kind=kOutput, calls=%fused_computation.8 | convolution fusion | flops 4312793088 | bytes 20996096 | tf_op jit(solution)/shard_map/dot_general | solution.py:22
  375.5 6.9 collective-permute-done.42
  388.0 47.6 %score.1 = (bf16[8,1000,2048]{2,1,0:T(8,128)(2,1)}, f32[8,1,2048]{2,1,0:T(1,128)S(1)}, f32[8,2048]{1,0:T(8,128)S(1)}, f32[256,2048]{1,0:T(8,128)S(1)}) custom-call(bf16[2048,256]{1,0:T(8,128)(2,1)S(1)} %bitcast.411, bf16[8,1000,256]{2,1,0:T(8,128)(2,1)} %pad_maximum_fusion.table_ref), custom_call_target="tpu_custom_call" | custom-call | tf_op jit(solution)/shard_map/score/pallas_call | solution.py:309
  486.3 19.0 %table_product.1.sum_ref = f32[8,1000,256]{2,1,0:T(8,128)} custom-call(bf16[8,1000,2048]{2,1,0:T(8,128)(2,1)} %get-tuple-element.36.raised_ref, bf16[2048,256]{1,0:T(8,128)(2,1)S(1)} %bitcast.412, f32[2048,8]{1,0:T(8,128)S(1)} %fusion.41.coef_ref), custom_call_target="tpu_custom_call" | custom-call | tf_op jit(solution)/shard_map/table_product/pallas_call | solution.py:350
  510.1 10.4 %fusion.158 = (bf16[2048]{0:T(1024)(128)(2,1)S(1)}, bf16[1024,2048]{1,0:T(8,128)(2,1)S(1)}) fusion(f32[1024,2048]{1,0:T(8,128)} %get-tuple-element.315, f32[2048]{0:T(1024)S(1)} %bitcast.500, bf16[2048,1024]{1,0:T(8,128)(2,1)S(1)} %bitcast.426, f32[1024,1024]{0,1:T(8,128)S(1)} %fusion.159, f32[]{:T(128)} %bitcast.25), kind=kOutput, calls=%fused_computation.559 | convolution fusion | flops 4326422528 | bytes 20983812 | tf_op jit(solution)/shard_map/dot_general | solution.py:26
  530.5 8.1 fusion.156
  539.1 8.2 convolution_convert_fusion.1
  553.0 24.3 %collective-permute-done.80 = bf16[4,2,2,32,2048]{4,3,2,1,0:T(8,128)(2,1)S(1)} collective-permute-done((bf16[4,2,2,32,2048]{4,3,2,1,0:T(8,128)(2,1)}, bf16[4,2,2,32,2048]{4,3,2,1,0:T(8,128)(2,1)S(1)}, u32[]{:S(2)}, u32[]{:S(2)}) %collective-permute-start.80) | collective-permute-done | bytes 2097184 | tf_op jit(solution)/shard_map/ppermute | solution.py:34
  582.5 6.3 multiply_add_fusion
  592.2 42.5 %attend_back.1 = (bf16[1024,512]{1,0:T(8,128)(2,1)S(1)}, bf16[1024,512]{1,0:T(8,128)(2,1)S(1)}, bf16[1024,512]{1,0:T(8,128)(2,1)S(1)}) custom-call(s32[4]{0:T(128)S(1)} %get-tuple-element.326.lo_ref, s32[4]{0:T(128)S(1)} %get-tuple-element.325.hi_ref, bf16[1024,512]{1,0:T(8,128)(2,1)S(1)} %fusion.8.q_ref, bf16[1024,512]{1,0:T(8,128)(2,1)S(1)} %get-tuple-element.216.k_ref, ...), custom_call_target="tpu_custom_call" | custom-call | tf_op jit(solution)/shard_map/attend_back/pallas_call | solution.py:250
  641.4 5.5 fusion.157
  649.4 7.0 collective-permute-done.76
  657.1 5.6 collective-permute-done.77
  662.7 6.7 collective-permute-done.78
  672.4 9.5 %collective-permute-done.82 = bf16[2,32,2048]{2,1,0:T(8,128)(2,1)S(1)} collective-permute-done((bf16[2,32,2048]{2,1,0:T(8,128)(2,1)S(1)}, bf16[2,32,2048]{2,1,0:T(8,128)(2,1)S(1)}, u32[]{:S(2)}, u32[]{:S(2)}) %collective-permute-start.82) | collective-permute-done | bytes 262176 | tf_op jit(solution)/shard_map/ppermute | solution.py:44
  687.7 5.5 collective-permute-done.83
  693.3 5.5 collective-permute-done.89
  732.6 5.4 collective-permute-done.54
  748.5 11.2 %table_add.1 = bf16[8,1000,256]{2,1,0:T(8,128)(2,1)S(1)} custom-call(f32[8,1000,256]{2,1,0:T(8,128)} %table_product.1.sum_ref, s32[1,2048]{1,0:T(1,128)S(1)} %compare_select_fusion.13.slot_ref, bf16[2048,256]{1,0:T(8,128)(2,1)S(1)} %bitcast.413), custom_call_target="tpu_custom_call" | custom-call | tf_op jit(solution)/shard_map/table_add/pallas_call | solution.py:376
  774.1 7.6 collective-permute-done.73
  789.8 9.7 %collective-permute-done.61 = bf16[2,504,256]{2,1,0:T(8,128)(2,1)S(1)} collective-permute-done((bf16[2,504,256]{2,1,0:T(8,128)(2,1)S(1)}, bf16[2,504,256]{2,1,0:T(8,128)(2,1)S(1)}, u32[]{:S(2)}, u32[]{:S(2)}) %collective-permute-start.61) | collective-permute-done | bytes 516128 | tf_op jit(solution)/shard_map/ppermute | solution.py:44
  808.9 7.1 collective-permute-done.58
  (596 shorter events, 394.6 us)
Async XLA Ops:
  2.8 29.3 %collective-permute-start = (s32[2050]{0:T(1024)S(1)}, s32[2050]{0:T(1024)S(1)}, u32[]{:S(2)}, u32[]{:S(2)}) collective-permute-start(s32[2050]{0:T(1024)S(1)} %concatenate.109), channel_id=1, source_target_pairs={{0,2},{2,0},{1,3},{3,1},{4,6},{6,4},{5,7},{7,5},{8,10},{10,8},{9,1... | collective-permute-start | bytes 24608 | tf_op jit(solution)/shard_map/ppermute | solution.py:34
  8.9 30.2 %collective-permute-start.12 = (bf16[80,256]{1,0:T(8,128)(2,1)}, bf16[80,256]{1,0:T(8,128)(2,1)}, u32[]{:S(2)}, u32[]{:S(2)}) collective-permute-start(bf16[80,256]{1,0:T(8,128)(2,1)} %maximum_maximum_fusion.1), channel_id=1, source_target_pairs={{0,2},{2,0},{1,3},{3,1},{4,6},{6,4},{5,7},{7,5},{8,10},{10,8},{9,1... | collective-permute-start | bytes 122888 | tf_op jit(solution)/shard_map/ppermute | solution.py:34
  9.0 32.1 %collective-permute-start.24 = (bf16[1,32,1024]{2,1,0:T(8,128)(2,1)}, bf16[1,32,1024]{2,1,0:T(8,128)(2,1)S(1)}, u32[]{:S(2)}, u32[]{:S(2)}) collective-permute-start(bf16[1,32,1024]{2,1,0:T(8,128)(2,1)} %bitcast.476), channel_id=1, source_target_pairs={{0,24},{8,0},{16,8},{24,16},{1,25},{9,1},{17,9},{25,17},{2,26},{10... | collective-permute-start | bytes 196616 | tf_op jit(solution)/shard_map/ppermute | solution.py:39
  17.4 34.6 %collective-permute-start.30 = (bf16[32,2048]{1,0:T(8,128)(2,1)}, bf16[32,2048]{1,0:T(8,128)(2,1)}, u32[]{:S(2)}, u32[]{:S(2)}) collective-permute-start(bf16[32,2048]{1,0:T(8,128)(2,1)} %bitcast.212), channel_id=1, source_target_pairs={{0,2},{2,0},{1,3},{3,1},{4,6},{6,4},{5,7},{7,5},{8,10},{10,8},{9,1... | collective-permute-start | bytes 393224 | tf_op jit(solution)/shard_map/ppermute | solution.py:34
  19.1 52.2 %collective-permute-start.1 = (bf16[1,496,256]{2,1,0:T(8,128)(2,1)}, bf16[1,496,256]{2,1,0:T(8,128)(2,1)}, u32[]{:S(2)}, u32[]{:S(2)}) collective-permute-start(bf16[1,496,256]{2,1,0:T(8,128)(2,1)} %slice_bitcast_fusion.13), channel_id=1, source_target_pairs={{0,24},{8,0},{16,8},{24,16},{1,25},{9,1},{17,9},{25,17},{2,26},{10... | collective-permute-start | bytes 761864 | tf_op jit(solution)/shard_map/ppermute | solution.py:39
  32.1 42.4 %collective-permute-start.5 = (bf16[1,504,256]{2,1,0:T(8,128)(2,1)}, bf16[1,504,256]{2,1,0:T(8,128)(2,1)}, u32[]{:S(2)}, u32[]{:S(2)}) collective-permute-start(bf16[1,504,256]{2,1,0:T(8,128)(2,1)} %slice_bitcast_fusion.8), channel_id=1, source_target_pairs={{0,4},{4,0},{1,5},{5,1},{2,6},{6,2},{3,7},{7,3},{8,12},{12,8},{9,1... | collective-permute-start | bytes 774152 | tf_op jit(solution)/shard_map/ppermute | solution.py:34
  39.1 37.5 %collective-permute-start.36 = (bf16[1,128,1024]{2,1,0:T(8,128)(2,1)S(1)}, bf16[1,128,1024]{2,1,0:T(8,128)(2,1)S(1)}, u32[]{:S(2)}, u32[]{:S(2)}) collective-permute-start(bf16[1,128,1024]{2,1,0:T(8,128)(2,1)S(1)} %bitcast.463), channel_id=1, source_target_pairs={{0,24},{8,0},{16,8},{24,16},{1,25},{9,1},{17,9},{25,17},{2,26},{10... | collective-permute-start | bytes 786440 | tf_op jit(solution)/shard_map/ppermute | solution.py:39
  51.9 31.4 %collective-permute-start.19 = (bf16[1,64,1536]{2,1,0:T(8,128)(2,1)S(1)}, bf16[1,64,1536]{2,1,0:T(8,128)(2,1)S(1)}, u32[]{:S(2)}, u32[]{:S(2)}) collective-permute-start(bf16[1,64,1536]{2,1,0:T(8,128)(2,1)S(1)} %bitcast.456), channel_id=1, source_target_pairs={{0,24},{8,0},{16,8},{24,16},{1,25},{9,1},{17,9},{25,17},{2,26},{10... | collective-permute-start | bytes 589832 | tf_op jit(solution)/shard_map/ppermute | solution.py:39
  76.6 30.1 %collective-permute-start.2 = (bf16[1,496,256]{2,1,0:T(8,128)(2,1)}, bf16[1,496,256]{2,1,0:T(8,128)(2,1)S(1)}, u32[]{:S(2)}, u32[]{:S(2)}) collective-permute-start(bf16[1,496,256]{2,1,0:T(8,128)(2,1)} %collective-permute-done.1), channel_id=1, source_target_pairs={{0,24},{8,0},{16,8},{24,16},{1,25},{9,1},{17,9},{25,17},{2,26},{10... | collective-permute-start | bytes 761864 | tf_op jit(solution)/shard_map/ppermute | solution.py:39
  79.8 49.7 %collective-permute-start.6 = (bf16[2,504,256]{2,1,0:T(8,128)(2,1)S(1)}, bf16[2,504,256]{2,1,0:T(8,128)(2,1)S(1)}, u32[]{:S(2)}, u32[]{:S(2)}) collective-permute-start(bf16[2,504,256]{2,1,0:T(8,128)(2,1)S(1)} %pad_maximum_fusion.9), channel_id=1, source_target_pairs={{0,24},{8,0},{16,8},{24,16},{1,25},{9,1},{17,9},{25,17},{2,26},{10... | collective-permute-start | bytes 1548296 | tf_op jit(solution)/shard_map/ppermute | solution.py:39
  106.7 30.1 %collective-permute-start.28 = (bf16[8,32,1024]{2,1,0:T(8,128)(2,1)S(1)}, bf16[8,32,1024]{2,1,0:T(8,128)(2,1)S(1)}, u32[]{:S(2)}, u32[]{:S(2)}) collective-permute-start(bf16[8,32,1024]{2,1,0:T(8,128)(2,1)S(1)} %get-tuple-element.251), channel_id=1, source_target_pairs={{0,4},{4,0},{1,5},{5,1},{2,6},{6,2},{3,7},{7,3},{8,12},{12,8},{9,1... | collective-permute-start | bytes 1572872 | tf_op jit(solution)/shard_map/ppermute | solution.py:34
  117.9 38.0 %collective-permute-start.17 = (bf16[8,160,256]{2,1,0:T(8,128)(2,1)}, bf16[8,160,256]{2,1,0:T(8,128)(2,1)}, u32[]{:S(2)}, u32[]{:S(2)}) collective-permute-start(bf16[8,160,256]{2,1,0:T(8,128)(2,1)} %get-tuple-element.233), channel_id=1, source_target_pairs={{0,1},{1,0},{2,3},{3,2},{4,5},{5,4},{6,7},{7,6},{8,9},{9,8},{10,11... | collective-permute-start | bytes 1966088 | tf_op jit(solution)/shard_map/ppermute | solution.py:34
  129.5 41.6 %collective-permute-start.4 = (bf16[4,496,256]{2,1,0:T(8,128)(2,1)}, bf16[4,496,256]{2,1,0:T(8,128)(2,1)}, u32[]{:S(2)}, u32[]{:S(2)}) collective-permute-start(bf16[4,496,256]{2,1,0:T(8,128)(2,1)} %pad_maximum_fusion.7), channel_id=1, source_target_pairs={{0,4},{4,0},{1,5},{5,1},{2,6},{6,2},{3,7},{7,3},{8,12},{12,8},{9,1... | collective-permute-start | bytes 3047432 | tf_op jit(solution)/shard_map/ppermute | solution.py:34
  134.3 59.2 %collective-permute-start.22 = (bf16[4,64,1536]{2,1,0:T(8,128)(2,1)}, bf16[4,64,1536]{2,1,0:T(8,128)(2,1)}, u32[]{:S(2)}, u32[]{:S(2)}) collective-permute-start(bf16[4,64,1536]{2,1,0:T(8,128)(2,1)} %pad_maximum_fusion.8), channel_id=1, source_target_pairs={{0,4},{4,0},{1,5},{5,1},{2,6},{6,2},{3,7},{7,3},{8,12},{12,8},{9,1... | collective-permute-start | bytes 2359304 | tf_op jit(solution)/shard_map/ppermute | solution.py:34
  136.8 59.6 %collective-permute-start.39 = (bf16[4,128,1024]{2,1,0:T(8,128)(2,1)}, bf16[4,128,1024]{2,1,0:T(8,128)(2,1)}, u32[]{:S(2)}, u32[]{:S(2)}) collective-permute-start(bf16[4,128,1024]{2,1,0:T(8,128)(2,1)} %pad_maximum_fusion.5), channel_id=1, source_target_pairs={{0,4},{4,0},{1,5},{5,1},{2,6},{6,2},{3,7},{7,3},{8,12},{12,8},{9,1... | collective-permute-start | bytes 3145736 | tf_op jit(solution)/shard_map/ppermute | solution.py:34
  141.6 31.8 %collective-permute-start.8 = (bf16[2,504,256]{2,1,0:T(8,128)(2,1)}, bf16[2,504,256]{2,1,0:T(8,128)(2,1)}, u32[]{:S(2)}, u32[]{:S(2)}) collective-permute-start(bf16[2,504,256]{2,1,0:T(8,128)(2,1)} %collective-permute-done.7), channel_id=1, source_target_pairs={{0,24},{8,0},{16,8},{24,16},{1,25},{9,1},{17,9},{25,17},{2,26},{10... | collective-permute-start | bytes 1548296 | tf_op jit(solution)/shard_map/ppermute | solution.py:39
  155.8 45.3 %collective-permute-start.34 = (bf16[4,64,2048]{2,1,0:T(8,128)(2,1)}, bf16[4,64,2048]{2,1,0:T(8,128)(2,1)}, u32[]{:S(2)}, u32[]{:S(2)}) collective-permute-start(bf16[4,64,2048]{2,1,0:T(8,128)(2,1)} %pad_maximum_fusion.4), channel_id=1, source_target_pairs={{0,1},{1,0},{2,3},{3,2},{4,5},{5,4},{6,7},{7,6},{8,9},{9,8},{10,11... | collective-permute-start | bytes 3145736 | tf_op jit(solution)/shard_map/ppermute | solution.py:34
  196.0 38.7 %collective-permute-start.23 = (bf16[8,64,1536]{2,1,0:T(8,128)(2,1)}, bf16[8,64,1536]{2,1,0:T(8,128)(2,1)S(1)}, u32[]{:S(2)}, u32[]{:S(2)}) collective-permute-start(bf16[8,64,1536]{2,1,0:T(8,128)(2,1)} %get-tuple-element.225), channel_id=1, source_target_pairs={{0,1},{1,0},{2,3},{3,2},{4,5},{5,4},{6,7},{7,6},{8,9},{9,8},{10,11... | collective-permute-start | bytes 4718600 | tf_op jit(solution)/shard_map/ppermute | solution.py:34
  199.3 103.7 %collective-permute-start.40 = (bf16[8,128,1024]{2,1,0:T(8,128)(2,1)}, bf16[8,128,1024]{2,1,0:T(8,128)(2,1)}, u32[]{:S(2)}, u32[]{:S(2)}) collective-permute-start(bf16[8,128,1024]{2,1,0:T(8,128)(2,1)} %get-tuple-element.221), channel_id=1, source_target_pairs={{0,1},{1,0},{2,3},{3,2},{4,5},{5,4},{6,7},{7,6},{8,9},{9,8},{10,11... | collective-permute-start | bytes 6291464 | tf_op jit(solution)/shard_map/ppermute | solution.py:34
  204.0 113.0 %collective-permute-start.35 = (bf16[8,64,2048]{2,1,0:T(8,128)(2,1)}, bf16[8,64,2048]{2,1,0:T(8,128)(2,1)}, u32[]{:S(2)}, u32[]{:S(2)}) collective-permute-start(bf16[8,64,2048]{2,1,0:T(8,128)(2,1)} %get-tuple-element.223), channel_id=1, source_target_pairs={{0,4},{4,0},{1,5},{5,1},{2,6},{6,2},{3,7},{7,3},{8,12},{12,8},{9,1... | collective-permute-start | bytes 6291464 | tf_op jit(solution)/shard_map/ppermute | solution.py:34
  302.7 36.8 %collective-permute-start.29 = (bf16[1024,1024]{0,1:T(8,128)(2,1)}, bf16[1024,1024]{0,1:T(8,128)(2,1)}, u32[]{:S(2)}, u32[]{:S(2)}) collective-permute-start(bf16[1024,1024]{0,1:T(8,128)(2,1)} %get-tuple-element.312), channel_id=1, source_target_pairs={{0,2},{2,0},{1,3},{3,1},{4,6},{6,4},{5,7},{7,5},{8,10},{10,8},{9,1... | collective-permute-start | bytes 6291464 | tf_op jit(solution)/shard_map/ppermute | solution.py:34
  383.8 54.1 %collective-permute-start.48 = (f32[2,512]{1,0:T(2,128)S(1)}, f32[2,512]{1,0:T(2,128)S(1)}, u32[]{:S(2)}, u32[]{:S(2)}) collective-permute-start(f32[2,512]{1,0:T(2,128)S(1)} %maximum_select_fusion.13), channel_id=1, source_target_pairs={{0,1},{1,0},{2,3},{3,2},{4,5},{5,4},{6,7},{7,6},{8,9},{9,8},{10,11... | collective-permute-start | bytes 12296 | tf_op jit(solution)/shard_map/ppermute | solution.py:34
  475.0 30.2 %collective-permute-start.46 = (f32[1024]{0:T(1024)S(1)}, f32[1024]{0:T(1024)S(1)}, u32[]{:S(2)}, u32[]{:S(2)}) collective-permute-start(f32[1024]{0:T(1024)S(1)} %sub.371), channel_id=1, source_target_pairs={{0,1},{1,0},{2,3},{3,2},{4,5},{5,4},{6,7},{7,6},{8,9},{9,8},{10,11... | collective-permute-start | bytes 12296 | tf_op jit(solution)/shard_map/ppermute | solution.py:34
  529.1 48.3 %collective-permute-start.80 = (bf16[4,2,2,32,2048]{4,3,2,1,0:T(8,128)(2,1)}, bf16[4,2,2,32,2048]{4,3,2,1,0:T(8,128)(2,1)S(1)}, u32[]{:S(2)}, u32[]{:S(2)}) collective-permute-start(bf16[4,2,2,32,2048]{4,3,2,1,0:T(8,128)(2,1)} %dynamic-slice_bitcast_fusion), channel_id=1, source_target_pairs={{0,4},{4,0},{1,5},{5,1},{2,6},{6,2},{3,7},{7,3},{8,12},{12,8},{9,1... | collective-permute-start | bytes 6291464 | tf_op jit(solution)/shard_map/ppermute | solution.py:34
  538.6 41.2 %collective-permute-start.52 = (bf16[1024,1024]{0,1:T(8,128)(2,1)}, bf16[1024,1024]{0,1:T(8,128)(2,1)S(1)}, u32[]{:S(2)}, u32[]{:S(2)}) collective-permute-start(bf16[1024,1024]{0,1:T(8,128)(2,1)} %get-tuple-element.319), channel_id=1, source_target_pairs={{0,2},{2,0},{1,3},{3,1},{4,6},{6,4},{5,7},{7,5},{8,10},{10,8},{9,1... | collective-permute-start | bytes 6291464 | tf_op jit(solution)/shard_map/ppermute | solution.py:34
  550.8 84.1 %collective-permute-start.86 = (bf16[4,2,128,1024]{3,2,0,1:T(8,128)(2,1)}, bf16[4,2,128,1024]{3,2,0,1:T(8,128)(2,1)}, u32[]{:S(2)}, u32[]{:S(2)}) collective-permute-start(bf16[4,2,128,1024]{3,2,0,1:T(8,128)(2,1)} %bitcast.398), channel_id=1, source_target_pairs={{0,1},{1,0},{2,3},{3,2},{4,5},{5,4},{6,7},{7,6},{8,9},{9,8},{10,11... | collective-permute-start | bytes 6291464 | tf_op jit(solution)/shard_map/ppermute | solution.py:34
  579.4 90.1 %collective-permute-start.81 = (bf16[4,2,32,2048]{3,2,1,0:T(8,128)(2,1)}, bf16[4,2,32,2048]{3,2,1,0:T(8,128)(2,1)}, u32[]{:S(2)}, u32[]{:S(2)}) collective-permute-start(bf16[4,2,32,2048]{3,2,1,0:T(8,128)(2,1)} %dynamic-slice_bitcast_fusion.3), channel_id=1, source_target_pairs={{0,1},{1,0},{2,3},{3,2},{4,5},{5,4},{6,7},{7,6},{8,9},{9,8},{10,11... | collective-permute-start | bytes 3145736 | tf_op jit(solution)/shard_map/ppermute | solution.py:34
  590.4 56.5 %collective-permute-start.75 = (bf16[4,2,32,1024]{3,2,0,1:T(8,128)(2,1)S(1)}, bf16[4,2,32,1024]{3,2,0,1:T(8,128)(2,1)S(1)}, u32[]{:S(2)}, u32[]{:S(2)}) collective-permute-start(bf16[4,2,32,1024]{3,2,0,1:T(8,128)(2,1)S(1)} %bitcast.471), channel_id=1, source_target_pairs={{0,4},{4,0},{1,5},{5,1},{2,6},{6,2},{3,7},{7,3},{8,12},{12,8},{9,1... | collective-permute-start | bytes 1572872 | tf_op jit(solution)/shard_map/ppermute | solution.py:34
  637.7 33.6 %collective-permute-start.87 = (bf16[4,128,1024]{2,1,0:T(8,128)(2,1)S(1)}, bf16[4,128,1024]{2,1,0:T(8,128)(2,1)S(1)}, u32[]{:S(2)}, u32[]{:S(2)}) collective-permute-start(bf16[4,128,1024]{2,1,0:T(8,128)(2,1)S(1)} %dynamic-slice_bitcast_fusion.2), channel_id=1, source_target_pairs={{0,4},{4,0},{1,5},{5,1},{2,6},{6,2},{3,7},{7,3},{8,12},{12,8},{9,1... | collective-permute-start | bytes 3145736 | tf_op jit(solution)/shard_map/ppermute | solution.py:34
  648.9 50.6 %collective-permute-start.69 = (bf16[4,2,2,32,1536]{4,3,2,1,0:T(8,128)(2,1)S(1)}, bf16[4,2,2,32,1536]{4,3,2,1,0:T(8,128)(2,1)S(1)}, u32[]{:S(2)}, u32[]{:S(2)}) collective-permute-start(bf16[4,2,2,32,1536]{4,3,2,1,0:T(8,128)(2,1)S(1)} %dynamic-slice_bitcast_fusion.1), channel_id=1, source_target_pairs={{0,1},{1,0},{2,3},{3,2},{4,5},{5,4},{6,7},{7,6},{8,9},{9,8},{10,11... | collective-permute-start | bytes 4718600 | tf_op jit(solution)/shard_map/ppermute | solution.py:34
  649.4 64.7 %collective-permute-start.53 = (bf16[1024,1024]{0,1:T(8,128)(2,1)}, bf16[1024,1024]{0,1:T(8,128)(2,1)S(1)}, u32[]{:S(2)}, u32[]{:S(2)}) collective-permute-start(bf16[1024,1024]{0,1:T(8,128)(2,1)} %get-tuple-element.321), channel_id=1, source_target_pairs={{0,2},{2,0},{1,3},{3,1},{4,6},{6,4},{5,7},{7,5},{8,10},{10,8},{9,1... | collective-permute-start | bytes 6291464 | tf_op jit(solution)/shard_map/ppermute | solution.py:34
  743.2 29.6 %collective-permute-start.72 = (bf16[2,32,1536]{2,1,0:T(8,128)(2,1)S(1)}, bf16[2,32,1536]{2,1,0:T(8,128)(2,1)S(1)}, u32[]{:S(2)}, u32[]{:S(2)}) collective-permute-start(bf16[2,32,1536]{2,1,0:T(8,128)(2,1)S(1)} %fusion.68), channel_id=1, source_target_pairs={{0,8},{8,16},{16,24},{24,0},{1,9},{9,17},{17,25},{25,1},{2,10},{10... | collective-permute-start | bytes 589832 | tf_op jit(solution)/shard_map/ppermute | solution.py:44
  (129 other events, 1846.6 us)
